TPU v7x, 32 devices: a whole 2x2x4 slice. The times are simulated.
32 devices in a mesh: dp: 2 (over core), ctx: 4 (over y, x), tp: 4 (over z).
Axes of the slice: x: 2, y: 2, z: 4, core: 2. Of those that a mesh axis runs over, the one named last changes fastest.
Arguments:
- inputs: bfloat16 [24, 1024, 512], P('dp', 'ctx'), may hold values from -6 to 6
- lengths: int32 [24], P('dp'), may hold values from 256 to 1024, as said below
- norm_gain: float32 [512], P('dp'), may hold values from 0.5 to 1.5
- skip_weight: float32 [512], P('dp'), may hold values from -3 to 3
- lambda_re: float32 [384], P(('tp', 'dp')), may hold values from -1 to -0.1
- lambda_im: float32 [384], P(('tp', 'dp')), may hold values from -20 to 20
- log_step: float32 [384], P(('tp', 'dp')), may hold values from -6.9 to -3
- b_re: bfloat16 [384, 512], P('tp', 'dp'), may hold values from -0.25 to 0.25
- b_im: bfloat16 [384, 512], P('tp', 'dp'), may hold values from -0.25 to 0.25
- c_re: bfloat16 [512, 384], P('dp', 'tp'), may hold values from -0.875 to 0.875
- c_im: bfloat16 [512, 384], P('dp', 'tp'), may hold values from -0.875 to 0.875
- glu_weight: bfloat16 [512, 512], P('dp', 'tp'), may hold values from -0.25 to 0.25
- glu_bias: float32 [512], P(('tp', 'dp')), may hold values from -3 to 3
- out_grad: bfloat16 [24, 1024, 512], P('dp', 'ctx', 'tp'), may hold values from -6 to 6
Outputs:
- output: bfloat16 [24, 1024, 512], P('dp', 'ctx', 'tp')
- input_grad: float32 [24, 1024, 512], P('dp', 'ctx', 'tp')
- grad_norm_gain: float32 [512], P('dp')
- grad_skip: float32 [512], P('dp')
- grad_lambda_re: float32 [384], P(('tp', 'dp'))
- grad_lambda_im: float32 [384], P(('tp', 'dp'))
- grad_log_step: float32 [384], P(('tp', 'dp'))
- grad_b_re: float32 [384, 512], P('tp', 'dp')
- grad_b_im: float32 [384, 512], P('tp', 'dp')
- grad_c_re: float32 [512, 384], P('dp', 'tp')
- grad_c_im: float32 [512, 384], P('dp', 'tp')
- grad_glu_weight: float32 [512, 512], P('dp', 'tp')
- grad_glu_bias: float32 [512], P(('tp', 'dp'))
Inputs may be any that keep to these rules, and one draw needn't show every extreme that they name: `lengths`: each sequence's valid length lies between 256 and 1024; some sequence has exactly 1024.
All inputs are finite; a program needn't handle non-finite values.
Results may differ from a plain program's by a relative error of at most 0.02.
Values may be sent and summed in bfloat16 or wider, within the bound.
A program may use at most 128 MiB of HBM per device.

v0:
```python
import functools

import jax
import jax.numpy as jnp
from jax import lax
from jax.experimental import pallas as pl
from jax.experimental.pallas import tpu as pltpu
from jax.sharding import PartitionSpec as P

epsilon = 1e-05


def carried_in(value, axis, combine, identity, reverse):
    count, index = (lax.axis_size(axis), lax.axis_index(axis))
    everything = jax.tree.map(lambda part: lax.all_gather(part, axis), value)
    start = jax.tree.map(
        lambda part, zero: jnp.broadcast_to(jnp.asarray(zero, part.dtype), part.shape),
        value,
        identity,
    )

    def lap(k, before):
        at = count - 1 - k if reverse else k
        reached = at > index if reverse else at < index
        new = combine(before, jax.tree.map(lambda part: part[at], everything))
        return jax.tree.map(lambda a, b: jnp.where(reached, a, b), new, before)

    return lax.fori_loop(0, count, lap, start)


def contract(left, right, left_dim, right_dim):
    return lax.dot_general(
        left, right, (((left_dim,), (right_dim,)), ((), ())), preferred_element_type=jnp.float32
    )


def combine(earlier, later):
    e_re, e_im, eb_re, eb_im = earlier
    l_re, l_im, lb_re, lb_im = later
    return (
        e_re * l_re - e_im * l_im,
        e_re * l_im + e_im * l_re,
        l_re * eb_re - l_im * eb_im + lb_re,
        l_re * eb_im + l_im * eb_re + lb_im,
    )


def discretize(lam_re, lam_im, step_log, mat_re, mat_im):
    step = jnp.exp(step_log)
    magnitude = jnp.exp(lam_re * step)
    decay_re = magnitude * jnp.cos(lam_im * step)
    decay_im = magnitude * jnp.sin(lam_im * step)
    denom = lam_re * lam_re + lam_im * lam_im
    coef_re = ((decay_re - 1.0) * lam_re + decay_im * lam_im) / denom
    coef_im = (decay_im * lam_re - (decay_re - 1.0) * lam_im) / denom
    bar_re = coef_re[:, None] * mat_re - coef_im[:, None] * mat_im
    bar_im = coef_re[:, None] * mat_im + coef_im[:, None] * mat_re
    return (decay_re, decay_im, jnp.concatenate([bar_re, bar_im], 0))


def normalize(tokens, gain):
    mean_val = jnp.mean(tokens, -1, keepdims=True)
    centered = tokens - mean_val
    var_val = jnp.mean(centered * centered, -1, keepdims=True)
    return centered * lax.rsqrt(var_val + epsilon) * gain


def powers(lam_re, lam_im, step_log, count):
    step = jnp.exp(step_log)
    exponent = (jnp.arange(count, dtype=jnp.float32) + 1.0)[:, None]
    magnitude = jnp.exp(exponent * lam_re * step)
    return (
        magnitude * jnp.cos(exponent * lam_im * step),
        magnitude * jnp.sin(exponent * lam_im * step),
    )


def on_device(
    inputs,
    lengths,
    norm_gain,
    skip_weight,
    lambda_re,
    lambda_im,
    log_step,
    b_re,
    b_im,
    c_re,
    c_im,
    glu_weight,
    glu_bias,
    out_grad,
):
    full_bre, full_bim, full_cre, full_cim, full_glu = (
        lax.all_gather(b_re, "dp", axis=1, tiled=True),
        lax.all_gather(b_im, "dp", axis=1, tiled=True),
        lax.all_gather(c_re, "dp", axis=0, tiled=True),
        lax.all_gather(c_im, "dp", axis=0, tiled=True),
        lax.all_gather(glu_weight, "dp", axis=0, tiled=True),
    )
    gain, skip_full, lam_re, lam_im, step_log, bias_vec = (
        lax.all_gather(norm_gain, "dp", axis=0, tiled=True),
        lax.all_gather(skip_weight, "dp", axis=0, tiled=True),
        lax.all_gather(lambda_re, "dp", axis=0, tiled=True),
        lax.all_gather(lambda_im, "dp", axis=0, tiled=True),
        lax.all_gather(log_step, "dp", axis=0, tiled=True),
        lax.all_gather(glu_bias, "dp", axis=0, tiled=True),
    )
    seq_count, blk_len, feat_dim = inputs.shape
    row_count = seq_count * blk_len
    state_count = full_bre.shape[0]
    unit_count = full_glu.shape[1]
    tp_rank = lax.axis_index("tp")
    unit_start = tp_rank * unit_count
    positions = lax.axis_index("ctx") * blk_len + jnp.arange(blk_len, dtype=jnp.int32)
    valid_mask = (positions[None, :] < lengths[:, None]).astype(jnp.float32).reshape(row_count, 1)
    tokens = inputs.astype(jnp.float32).reshape(row_count, feat_dim)
    tokens_mine = lax.dynamic_slice_in_dim(tokens, unit_start, unit_count, 1)
    cotangent = out_grad.astype(jnp.float32).reshape(row_count, unit_count)
    normed_f, norm_pull = jax.vjp(normalize, tokens, gain)
    normed_b = normed_f.astype(jnp.bfloat16)
    normed_r = normed_b.astype(jnp.float32)
    (decay_re, decay_im, bar_full), disc_pull = jax.vjp(
        discretize,
        lam_re,
        lam_im,
        step_log,
        full_bre.astype(jnp.float32),
        full_bim.astype(jnp.float32),
    )
    bar_b = bar_full.astype(jnp.bfloat16)
    drive = contract(normed_b, bar_b, 1, 1).reshape(seq_count, blk_len, 2 * state_count)
    full_re = jnp.broadcast_to(decay_re, (seq_count, blk_len, state_count))
    full_im = jnp.broadcast_to(decay_im, (seq_count, blk_len, state_count))
    local_states = lax.associative_scan(
        combine, (full_re, full_im, drive[..., :state_count], drive[..., state_count:]), axis=1
    )
    pow_re, pow_im = powers(lam_re, lam_im, step_log, blk_len)
    identity = (
        jnp.ones((1, state_count), jnp.float32),
        jnp.zeros((1, state_count), jnp.float32),
        jnp.zeros((seq_count, state_count), jnp.float32),
        jnp.zeros((seq_count, state_count), jnp.float32),
    )
    incoming = carried_in(
        (pow_re[-1:], pow_im[-1:], local_states[2][:, -1], local_states[3][:, -1]),
        "ctx",
        combine,
        identity,
        False,
    )
    in_re = incoming[2][:, None, :]
    in_im = incoming[3][:, None, :]
    state_re = local_states[2] + pow_re * in_re - pow_im * in_im
    state_im = local_states[3] + pow_re * in_im + pow_im * in_re
    states_b = (
        jnp.concatenate([state_re, state_im], -1)
        .reshape(row_count, 2 * state_count)
        .astype(jnp.bfloat16)
    )
    c_stack = jnp.concatenate([full_cre, -full_cim], 1)
    ssm_part = contract(states_b, c_stack, 1, 1)
    ssm_full = lax.psum(ssm_part.astype(jnp.bfloat16), "tp").astype(jnp.float32)
    pre_full = ssm_full + skip_full * normed_r
    gelu_full, gelu_pull = jax.vjp(jax.nn.gelu, pre_full)
    gelu_b = gelu_full.astype(jnp.bfloat16)
    gelu_part = lax.dynamic_slice_in_dim(gelu_b, unit_start, unit_count, 1)
    gelu_mine = gelu_part.astype(jnp.float32)
    gate = contract(gelu_b, full_glu, 1, 0) + bias_vec
    gate_sig = jax.nn.sigmoid(gate)
    output = (
        (valid_mask * (tokens_mine + gelu_mine * gate_sig))
        .astype(jnp.bfloat16)
        .reshape(seq_count, blk_len, unit_count)
    )
    branch_grad = valid_mask * cotangent
    gate_grad = branch_grad * gelu_mine * gate_sig * (1.0 - gate_sig)
    bias_grad = jnp.sum(gate_grad, 0)
    gate_b = gate_grad.astype(jnp.bfloat16)
    glu_grad = contract(gelu_b, gate_b, 0, 0)
    gelu_grad = contract(gate_b, full_glu, 1, 1)
    own_cols = (
        lax.dynamic_slice_in_dim(gelu_grad, unit_start, unit_count, 1) + branch_grad * gate_sig
    )
    gelu_grad = lax.dynamic_update_slice_in_dim(gelu_grad, own_cols, unit_start, 1)
    gelu_back = lax.psum(gelu_grad, "tp")
    (pre_grad,) = gelu_pull(gelu_back)
    skip_grad = jnp.sum(pre_grad * normed_r, 0)
    pre_b = pre_grad.astype(jnp.bfloat16)
    state_grad = contract(pre_b, c_stack, 1, 0).reshape(seq_count, blk_len, 2 * state_count)
    c_grad = contract(pre_b, states_b, 0, 0)
    back_local = lax.associative_scan(
        combine,
        (full_re, -full_im, state_grad[..., :state_count], state_grad[..., state_count:]),
        axis=1,
        reverse=True,
    )
    later_adj = carried_in(
        (pow_re[-1:], -pow_im[-1:], back_local[2][:, 0], back_local[3][:, 0]),
        "ctx",
        combine,
        identity,
        True,
    )
    rev_re = pow_re[::-1]
    rev_im = -pow_im[::-1]
    next_re = later_adj[2][:, None, :]
    next_im = later_adj[3][:, None, :]
    adj_re = back_local[2] + rev_re * next_re - rev_im * next_im
    adj_im = back_local[3] + rev_re * next_im + rev_im * next_re
    prev_re = jnp.concatenate([in_re, state_re[:, :-1]], 1)
    prev_im = jnp.concatenate([in_im, state_im[:, :-1]], 1)
    decay_grad_re = jnp.sum(adj_re * prev_re + adj_im * prev_im, (0, 1))
    decay_grad_im = jnp.sum(adj_im * prev_re - adj_re * prev_im, (0, 1))
    adj_b = (
        jnp.concatenate([adj_re, adj_im], -1)
        .reshape(row_count, 2 * state_count)
        .astype(jnp.bfloat16)
    )
    bar_grad = contract(adj_b, normed_b, 0, 0)
    normed_part = contract(adj_b, bar_b, 1, 0)
    normed_sum = lax.psum(normed_part.astype(jnp.bfloat16), "tp").astype(jnp.float32)
    normed_grad = normed_sum + skip_full * pre_grad
    token_grad, gain_grad = norm_pull(normed_grad)
    input_grad = (
        valid_mask * cotangent + lax.dynamic_slice_in_dim(token_grad, unit_start, unit_count, 1)
    ).reshape(seq_count, blk_len, unit_count)
    grad_cre = c_grad[:, :state_count]
    grad_cim = -c_grad[:, state_count:]
    lre_grad, lim_grad, step_grad, bre_grad, bim_grad = disc_pull(
        (decay_grad_re, decay_grad_im, bar_grad)
    )
    shards = (
        lax.psum_scatter(
            gain_grad.astype(jnp.bfloat16), "dp", scatter_dimension=0, tiled=True
        ).astype(jnp.float32),
        lax.psum_scatter(
            skip_grad.astype(jnp.bfloat16), "dp", scatter_dimension=0, tiled=True
        ).astype(jnp.float32),
        lax.psum_scatter(
            lre_grad.astype(jnp.bfloat16), "dp", scatter_dimension=0, tiled=True
        ).astype(jnp.float32),
        lax.psum_scatter(
            lim_grad.astype(jnp.bfloat16), "dp", scatter_dimension=0, tiled=True
        ).astype(jnp.float32),
        lax.psum_scatter(
            step_grad.astype(jnp.bfloat16), "dp", scatter_dimension=0, tiled=True
        ).astype(jnp.float32),
        lax.psum_scatter(
            bias_grad.astype(jnp.bfloat16), "dp", scatter_dimension=0, tiled=True
        ).astype(jnp.float32),
        lax.psum_scatter(
            bre_grad.astype(jnp.bfloat16), "dp", scatter_dimension=1, tiled=True
        ).astype(jnp.float32),
        lax.psum_scatter(
            bim_grad.astype(jnp.bfloat16), "dp", scatter_dimension=1, tiled=True
        ).astype(jnp.float32),
        lax.psum_scatter(
            grad_cre.astype(jnp.bfloat16), "dp", scatter_dimension=0, tiled=True
        ).astype(jnp.float32),
        lax.psum_scatter(
            grad_cim.astype(jnp.bfloat16), "dp", scatter_dimension=0, tiled=True
        ).astype(jnp.float32),
        lax.psum_scatter(
            glu_grad.astype(jnp.bfloat16), "dp", scatter_dimension=0, tiled=True
        ).astype(jnp.float32),
    )
    summed = (
        lax.psum(shards[0].astype(jnp.bfloat16), "ctx").astype(jnp.float32),
        lax.psum(shards[1].astype(jnp.bfloat16), "ctx").astype(jnp.float32),
        lax.psum(shards[2].astype(jnp.bfloat16), "ctx").astype(jnp.float32),
        lax.psum(shards[3].astype(jnp.bfloat16), "ctx").astype(jnp.float32),
        lax.psum(shards[4].astype(jnp.bfloat16), "ctx").astype(jnp.float32),
        lax.psum(shards[5].astype(jnp.bfloat16), "ctx").astype(jnp.float32),
        lax.psum(shards[6].astype(jnp.bfloat16), "ctx").astype(jnp.float32),
        lax.psum(shards[7].astype(jnp.bfloat16), "ctx").astype(jnp.float32),
        lax.psum(shards[8].astype(jnp.bfloat16), "ctx").astype(jnp.float32),
        lax.psum(shards[9].astype(jnp.bfloat16), "ctx").astype(jnp.float32),
        lax.psum(shards[10].astype(jnp.bfloat16), "ctx").astype(jnp.float32),
    )
    return (
        output,
        input_grad,
        summed[0],
        summed[1],
        summed[2],
        summed[3],
        summed[4],
        summed[6],
        summed[7],
        summed[8],
        summed[9],
        summed[10],
        summed[5],
    )


MESH = pl.DeviceIdType.MESH
SQ2PI = 0.7978845608028654


def nt(a, b):
    return lax.dot_general(a, b, (((1,), (1,)), ((), ())), preferred_element_type=jnp.float32)


def nn(a, b):
    return lax.dot_general(a, b, (((1,), (0,)), ((), ())), preferred_element_type=jnp.float32)


def tn(a, b):
    return lax.dot_general(a, b, (((0,), (0,)), ((), ())), preferred_element_type=jnp.float32)


def cmul(ar, ai, br, bi):
    return ar * br - ai * bi, ar * bi + ai * br


def lane(start, size):
    return pl.ds(pl.multiple_of(start, 128), size)


def fused_body(geo, *refs):
    D, C, T, S, L, H, N, U = geo
    R = S * L
    NS = N // T
    HD = H // D
    f32, bf16 = jnp.float32, jnp.bfloat16
    (len_ref, x_hbm, og_hbm, bre, bim, cre, cim, glu_hbm, gain_h, skip_h, lre_h, lim_h, stp_h, bias_h,
     out_hbm, tg_hbm, fc_ref, fg_ref, fb_ref, fv_ref) = refs[:20]
    (xv, nrm, xh, rs, raw, st, sb, tmp, act, gp, sig, ogv, ob, gl, pg, plb, mu, nb, tgb,
     xe, nrme, rawe, sbe, acte, tmpe, obe,
     w4, gt, smr, cst, ce, cer, cin, gc, gg, gb, r1c, r1g, r1b, s1c, s1g, s1b, r2c, r2g, r2b,
     s2c, s2g, s2b, r3c, r3g, r3b, s3c, s3g, s3b, r4c, r4g, r4b,
     vv, vr1, vr2, vr3, vf, accv, pk, sm_ref, glu, gain_in, skip_in, lre_in, lim_in, stp_in, bias_in,
     lsem, ssem, rsem) = refs[20:]
    d, c, t = lax.axis_index("dp"), lax.axis_index("ctx"), lax.axis_index("tp")
    half = t // 2
    t1 = t + 1 - 2 * lax.rem(t, 2)
    t2 = t + 2 - 4 * half
    t3 = T - 1 - t
    z1, z2, z3 = (d, c, t1), (d, c, t2), (d, c, t3)
    zpeer = [(d, c, lax.rem(t + k, T)) for k in range(1, T)]
    cpeer = [(d, lax.rem(c + k, C), t) for k in range(1, C)]
    sib = (1 - d, c, t)
    xpeer = [(1 - d, c, lax.rem(t + k, T)) for k in range(1, T)]
    everyone = zpeer + cpeer + [sib] + xpeer
    erank = [t2, t3]

    count = [0]
    started = []

    def remote(src, dst, peer):
        i = count[0]
        count[0] += 1
        cp = pltpu.make_async_remote_copy(
            src_ref=src, dst_ref=dst, send_sem=ssem.at[i], recv_sem=rsem.at[i],
            device_id=peer, device_id_type=MESH)
        cp.start()
        started.append(cp)
        return cp

    def arrived(*cps):
        for cp in cps:
            cp.wait_recv()

    nlocal = [0]

    def local(src, dst):
        cp = pltpu.make_async_copy(src, dst, lsem.at[nlocal[0]])
        nlocal[0] += 1
        cp.start()
        return cp

    def rows_at(start, size):
        return pl.ds(pl.multiple_of(start, size), size)

    barrier = pltpu.get_barrier_semaphore()
    for p in everyone:
        pl.semaphore_signal(barrier, inc=1, device_id=p, device_id_type=MESH)
    cp_small = [local(a, b) for a, b in (
        (lre_h, lre_in), (lim_h, lim_in), (stp_h, stp_in), (bias_h, bias_in), (gain_h, gain_in), (skip_h, skip_in))]
    mine = rows_at(R * t, R)
    cp_pk = [local(a, pk.at[k]) for k, a in enumerate((bre, bim, cre, cim))] + [local(glu_hbm, glu)]
    cx = local(x_hbm.at[mine], xv)
    cxe = [local(x_hbm.at[rows_at(R * e, R)], xe.at[pl.ds(R * k, R)]) for k, e in enumerate(erank)]
    co = local(og_hbm.at[mine], ogv.at[:, lane(U * t, U)])
    dl = lane(HD * d, HD)
    dr_ = rows_at(HD * d, HD)
    tl = lane(U * t, U)
    sm_ref[...] = jnp.zeros_like(sm_ref)
    for cp in cp_small:
        cp.wait()
    own = coefficients(lre_in[...], lim_in[...], stp_in[...])
    for k in range(4):
        sm_ref[k:k + 1, 0:NS // D] = own[k]
    sm_ref[4:5, 0:U // D] = bias_in[...]
    sm_ref[5:6, :] = gain_in[...]
    sm_ref[6:7, :] = skip_in[...]
    me8 = d * T + t
    smr[me8] = sm_ref[...]
    accv[...] = jnp.zeros_like(accv)
    vv[...] = jnp.zeros_like(vv)
    for cp in cp_pk:
        cp.wait()
    for k in range(4):
        w4[k, t, :, dl] = pk[k]
    gt[dr_, tl] = glu[...]
    cx.wait()

    def standard(x):
        cen = x - jnp.mean(x, -1, keepdims=True)
        rstd = lax.rsqrt(jnp.mean(cen * cen, -1, keepdims=True) + epsilon)
        return cen * rstd, rstd

    def ln_tile(i, _):
        for u in range(4):
            rows = rows_at(i * 128 + u * 32, 32)
            xn, rstd = standard(xv[rows, :].astype(f32))
            xh[rows, :] = xn
            rs[rows, :] = jnp.broadcast_to(rstd, (32, 128))
        return 0

    lax.fori_loop(0, R // 128, ln_tile, 0)
    pl.semaphore_wait(barrier, len(everyone))

    gq, hq = c // 2, lax.rem(c, 2)
    ql = lane(128 * hq, 128)
    wl = lane(HD * d + 128 * hq, 128)
    uq = HD // C
    gown = rows_at(uq * c, uq)
    grow = rows_at(HD * d + uq * c, uq)
    pair = rows_at(2 - 2 * half, 2)
    pairl = lane(2 * U * (1 - half), 2 * U)

    def first(k):
        q = 2 * k + gq
        return [remote(pk.at[q, :, ql], w4.at[q, t, :, wl], p) for p in (z1, z2)]

    small = [remote(sm_ref, smr.at[me8], p) for p in zpeer + [sib] + xpeer]
    w1b = first(0)
    w3b = [remote(pk.at[0:2], w4.at[0:2, t, :, dl], sib)]

    def pass_on(cp, blk):
        arrived(cp)
        return remote(blk, blk, z1)

    def spread(blk, *cps):
        arrived(*cps)
        return [remote(blk, blk, p) for p in cpeer]

    qb, qc = gq, 2 + gq
    gl1, gl2 = lane(U * t1, U), lane(U * t2, U)
    w1b3 = pass_on(w1b[1], w4.at[qb, t2, :, wl])
    w2b = [spread(w4.at[qb, t1, :, wl], w1b[0])]
    w1c = first(1)
    w1g = [remote(glu.at[gown], gt.at[grow, tl], p) for p in (z1, z2)]
    w3c = [remote(pk.at[2:4], w4.at[2:4, t, :, dl], sib)]
    w3g = [remote(glu, gt.at[dr_, tl], sib)]

    def cot_send(s):
        return [remote(og_hbm.at[rows_at(R * p[2] + L * s, L)], ogv.at[pl.ds(L * s, L), tl], p) for p in zpeer]

    arrived(*small)
    zero = jnp.zeros((8, H - HD), f32)
    vec = jnp.zeros((8, H), f32)
    bias = jnp.zeros((8, H), f32)
    for dd in range(D):
        for tt in range(T):
            ext = jnp.concatenate([smr[dd * T + tt], zero], 1)
            place = tt * D + dd
            vec = vec + (pltpu.roll(ext, place * (NS // D), 1) if place else ext)
            bias = bias + (pltpu.roll(ext, place * (U // D), 1) if place else ext)
    both = jnp.concatenate([smr[t], smr[T + t]], 1)
    gain_r, skip_r, bias_r = both[5:6, :], both[6:7, :], bias[4:5, :]

    w2b.append(spread(w4.at[qb, pair, :, wl], w1b3))
    row8 = lax.broadcasted_iota(jnp.int32, (8, N), 0)
    full = lambda v, k, n: jnp.broadcast_to(v[k:k + 1, :n], (8, n))
    dr, di = full(vec, 0, N), full(vec, 1, N)
    cr, ci = full(vec, 2, N), full(vec, 3, N)
    pows = {1: (dr, di)}
    for k in range(2, 9):
        pows[k] = cmul(*pows[k - 1], dr, di)
    for n_, k in ((0, 1), (1, 2), (2, 4)):
        keep = row8 >= k
        cst[2 * n_] = jnp.where(keep, pows[k][0], 0.0)
        cst[2 * n_ + 1] = jnp.where(keep, pows[k][1], 0.0)
        keep = row8 < 8 - k
        cst[8 + 2 * n_] = jnp.where(keep, pows[k][0], 0.0)
        cst[8 + 2 * n_ + 1] = jnp.where(keep, -pows[k][1], 0.0)
    pr, pi, qr, qi = pows[1][0], pows[1][1], pows[8][0], -pows[8][1]
    for r in range(1, 8):
        pr = jnp.where(row8 == r, pows[r + 1][0], pr)
        pi = jnp.where(row8 == r, pows[r + 1][1], pi)
        qr = jnp.where(row8 == r, pows[8 - r][0], qr)
        qi = jnp.where(row8 == r, -pows[8 - r][1], qi)
    cst[6], cst[7], cst[14], cst[15] = pr, pi, qr, qi
    cst[16], cst[17] = pows[8]
    cst[18], cst[19] = cr, ci
    big = pows[8]
    n_ = 8
    while n_ < L:
        big = cmul(*big, *big)
        n_ *= 2
    cst[20], cst[21] = big

    def nrm_tile(i, _):
        rows = rows_at(i * 32, 32)
        nrm[rows, :] = (xh[rows, :] * gain_r).astype(bf16)
        return 0

    lax.fori_loop(0, R // 32, nrm_tile, 0)
    w1c3 = pass_on(w1c[1], w4.at[qc, t2, :, wl])
    w2c = [spread(w4.at[qc, t1, :, wl], w1c[0])]
    w1g3 = pass_on(w1g[1], gt.at[grow, gl2])
    w2g = [spread(gt.at[grow, gl1], w1g[0])]
    og = [cot_send(0)]

    def lne_tile(i, _):
        for u in range(4):
            rows = rows_at(i * 128 + u * 32, 32)
            nrme[rows, :] = (standard(xe[rows, :].astype(f32))[0] * gain_r).astype(bf16)
        return 0

    for cp in cxe:
        cp.wait()
    lax.fori_loop(0, R // 128, lne_tile, 0)
    w2c.append(spread(w4.at[qc, pair, :, wl], w1c3))
    w2g.append(spread(gt.at[grow, pairl], w1g3))
    og.append(cot_send(1))
    arrived(*w2b[0])
    w3b.append(remote(w4.at[0:2, t1, :, dl], w4.at[0:2, t1, :, dl], sib))
    og.append(cot_send(2))
    lax.fori_loop(R // 128, 2 * R // 128, lne_tile, 0)
    arrived(*w2b[1])
    w3b.append(remote(w4.at[0:2, pair, :, dl], w4.at[0:2, pair, :, dl], sib))

    def seq_rows(s):
        return rows_at(s * L, L)

    def drive(src, dst, lo, hi, off):
        def step(s, _):
            dst[seq_rows(s), :] = nt(src[seq_rows(s + off), :], w4[0:2].reshape(2 * N, H))
            return 0

        lax.fori_loop(lo, hi, step, 0)

    def scan(src, dst, groups, base, coef, reverse):
        e = 0 if reverse else 7

        def tile(i, carry):
            carry = list(carry)
            ii = L // 32 - 1 - i if reverse else i
            for g, (rb, l0) in enumerate(groups):
                lr_, li_ = lane(l0, 128), lane(N + l0, 128)
                con = [cst[base + k, :, lr_] for k in range(8)]
                e0 = cst[16, :, lr_]
                e1 = -cst[17, :, lr_] if reverse else cst[17, :, lr_]
                loc = []
                for u in range(4):
                    uu = 3 - u if reverse else u
                    rows = rows_at(rb + ii * 32 + uu * 8, 8)
                    ar, ai = src[rows, lr_], src[rows, li_]
                    if coef:
                        ar, ai = cmul(cst[18, :, lr_], cst[19, :, lr_], ar, ai)
                    else:
                        ai = -ai
                    for n_, k in ((0, 1), (1, 2), (2, 4)):
                        sh = 8 - k if reverse else k
                        br, bi = pltpu.roll(ar, sh, 0), pltpu.roll(ai, sh, 0)
                        mr, mi = con[2 * n_], con[2 * n_ + 1]
                        ar, ai = ar + mr * br - mi * bi, ai + mr * bi + mi * br
                    loc.append((rows, ar, ai))
                kr, ki = carry[2 * g], carry[2 * g + 1]
                for rows, ar, ai in loc:
                    dst[rows, lr_] = ar + con[6] * kr - con[7] * ki
                    dst[rows, li_] = ai + con[6] * ki + con[7] * kr
                    endr = jnp.broadcast_to(ar[e:e + 1, :], (8, 128))
                    endi = jnp.broadcast_to(ai[e:e + 1, :], (8, 128))
                    kr, ki = endr + e0 * kr - e1 * ki, endi + e0 * ki + e1 * kr
                carry[2 * g], carry[2 * g + 1] = kr, ki
            return tuple(carry)

        z = jnp.zeros((8, 128), f32)
        return lax.fori_loop(0, L // 32, tile, (z,) * (2 * len(groups)))

    def scan_batch(src, dst, slot):
        def lanes_step(j, _):
            fin = scan(src, dst, [(s * L, 128 * j) for s in range(S)], 0, True, False)
            for s in range(S):
                ce[slot, pl.ds(s, 1), lane(128 * j, 128)] = fin[2 * s][0:1, :]
                ce[slot, pl.ds(S + s, 1), lane(128 * j, 128)] = fin[2 * s + 1][0:1, :]
            return 0

        lax.fori_loop(0, N // 128, lanes_step, 0)
        return [remote(ce.at[slot], cer.at[slot, k], p) for k, p in enumerate(cpeer)]

    def incoming(slot, cps, n, forward):
        arrived(*cps)
        bg = (cst[20, 0:1, :], cst[21, 0:1, :])
        wt = (jnp.ones((1, N), f32), jnp.zeros((1, N), f32))
        accr = jnp.zeros((n, N), f32)
        acci = jnp.zeros((n, N), f32)
        for k in range(1, C):
            got = cer[slot, k - 1] if forward else cer[slot, C - 1 - k]
            has = (c >= k) if forward else (c + k < C)
            w = jnp.where(has, 1.0, 0.0)
            wi = wt[1] if forward else -wt[1]
            ur, ui = cmul(wt[0], wi, got[0:n, :], got[n:2 * n, :])
            accr = accr + w * ur
            acci = acci + w * ui
            wt = cmul(*wt, *bg)
        cin[slot, 0:n, :] = accr
        cin[slot, n:2 * n, :] = acci

    def entering(slot, k, lanes):
        return jnp.broadcast_to(cin[slot, pl.ds(k, 1), lanes], (8, 128))

    def fix_batch(ref, dst, slot, keep):
        def fix_lanes(j, _):
            lr_, li_ = lane(128 * j, 128), lane(N + 128 * j, 128)
            p0, p1 = cst[6, :, lr_], cst[7, :, lr_]
            e0, e1 = cst[16, :, lr_], cst[17, :, lr_]
            q0 = tuple(entering(slot, k * S + s, lr_) for s in range(S) for k in range(2))

            def tile(i, q):
                q = list(q)
                for s in range(S):
                    rr, ri = [], []
                    for h in range(2):
                        rows = rows_at(s * L + i * 16 + 8 * h, 8)
                        vr, vi = cmul(p0, p1, q[2 * s], q[2 * s + 1])
                        ar, ai = ref[rows, lr_] + vr, ref[rows, li_] + vi
                        if keep:
                            ref[rows, lr_] = ar
                            ref[rows, li_] = ai
                        rr.append(ar)
                        ri.append(ai)
                        q[2 * s], q[2 * s + 1] = cmul(q[2 * s], q[2 * s + 1], e0, e1)
                    rows = rows_at(s * L + i * 16, 16)
                    dst[rows, lr_] = jnp.concatenate(rr, 0).astype(bf16)
                    dst[rows, li_] = (-jnp.concatenate(ri, 0)).astype(bf16)
                return tuple(q)

            lax.fori_loop(0, L // 16, tile, q0)
            return 0

        lax.fori_loop(0, N // 128, fix_lanes, 0)

    def each_seq(f):
        def step(s, _):
            f(seq_rows(s))
            return 0

        lax.fori_loop(0, S, step, 0)

    def tiles(f, lo=0, hi=R // 32):
        def step(i, _):
            f(i, rows_at(i * 32, 32))
            return 0

        lax.fori_loop(lo, hi, step, 0)

    def valid_of(i, rank):
        s = i // (L // 32)
        pos = c * L + lax.rem(i, L // 32) * 32 + lax.broadcasted_iota(jnp.int32, (32, 1), 0)
        return jnp.where(pos < len_ref[S * rank + s], 1.0, 0.0)

    def logistic(v):
        return 0.5 + 0.5 * jnp.tanh(0.5 * v)

    arrived(*w3b)
    drive(nrm, raw, 0, S, 0)
    fce = [scan_batch(raw, st, 0)]
    arrived(*w2c[0])
    w3c.append(remote(w4.at[2:4, t1, :, dl], w4.at[2:4, t1, :, dl], sib))
    arrived(*w2c[1])
    w3c.append(remote(w4.at[2:4, pair, :, dl], w4.at[2:4, pair, :, dl], sib))
    arrived(*w2g[0], *w2g[1])
    blk = gt.at[dr_, lane(U * t1, U)]
    w3g.append(remote(blk, blk, sib))
    blk = gt.at[dr_, pairl]
    w3g.append(remote(blk, blk, sib))

    def extra_start(k):
        drive(nrme, rawe.at[k], 0, S, S * k)
        fce.append(scan_batch(rawe.at[k], rawe.at[k], 1 + k))

    extra_start(0)
    incoming(0, fce[0], S, True)
    fix_batch(st, sb, 0, True)
    arrived(*w3c)

    def ssm_own(rows):
        tmp[rows, :] = nn(sb[rows, :], w4[2:4].reshape(2 * N, H))

    each_seq(ssm_own)

    def gelu_tile(i, rows):
        pre = tmp[rows, :] + skip_r * nrm[rows, :].astype(f32)
        sq = pre * pre
        th = jnp.tanh(pre * (SQ2PI + (SQ2PI * 0.044715) * sq))
        hf = 0.5 + 0.5 * th
        act[rows, :] = (pre * hf).astype(bf16)
        gp[rows, :] = hf + 0.5 * pre * (1.0 - th * th) * (SQ2PI + (3 * 0.044715 * SQ2PI) * sq)

    tiles(gelu_tile)
    arrived(*w3g)

    def gate_own(rows):
        tmp[rows, :] = nn(act[rows, :], gt[...])

    each_seq(gate_own)

    def out_tile(i, rows):
        sg = logistic(tmp[rows, :] + bias_r)
        sig[rows, :] = sg
        o = valid_of(i, t) * (xv[rows, :].astype(f32) + act[rows, :].astype(f32) * sg)
        ob[rows, :] = o.astype(bf16)

    tiles(out_tile)
    outc = [remote(ob.at[:, lane(U * t1, U)], out_hbm.at[mine, :], z1)]
    locals_ = [local(ob.at[:, tl], out_hbm.at[mine, :])]

    def fold(v):
        return jnp.sum(v.reshape(4, 8, v.shape[-1]), 0)

    def seq_tiles(s, f):
        def step(i, acc):
            return acc + fold(f(i, rows_at(i * 32, 32)))

        return lax.fori_loop(s * (L // 32), (s + 1) * (L // 32), step, jnp.zeros((8, H), f32))

    co.wait()

    def gate_tile(i, rows):
        sg = sig[rows, :]
        direct = valid_of(i, t) * ogv[rows, :].astype(f32) * sg
        g = direct * act[rows, :].astype(f32) * (1.0 - sg)
        gl[rows, :] = g.astype(bf16)
        sig[rows, :] = direct
        return g

    def pre_tile(i, rows):
        p = (tmp[rows, :] + sig[rows, :]) * gp[rows, :]
        pg[rows, :] = p
        plb[rows, :] = p.astype(bf16)
        return p * nrm[rows, :].astype(f32)

    def back_one(s):
        arrived(*og[s])
        rows = pl.ds(s * L, L)
        accv[0] += seq_tiles(s, gate_tile)
        tmp[rows, :] = nt(gl[rows, :], gt[...])
        accv[1] += seq_tiles(s, pre_tile)
        mu[rows, :] = nt(plb[rows, :], w4[2:4].reshape(2 * N, H))
        fin = scan(mu, mu, [(s * L, 128 * j) for j in range(N // 128)], 8, False, True)
        for j in range(N // 128):
            ce[3 + s, 0:1, 128 * j:128 * j + 128] = fin[2 * j][0:1, :]
            ce[3 + s, 1:2, 128 * j:128 * j + 128] = fin[2 * j + 1][0:1, :]
        return [remote(ce.at[3 + s], cer.at[3 + s, k], p) for k, p in enumerate(cpeer)]

    row1 = lax.broadcasted_iota(jnp.int32, (8, 128), 0)

    def back_two(s, cps):
        incoming(3 + s, cps, 1, False)
        nj = N // 128
        q0 = tuple(entering(3 + s, k, lane(128 * j, 128)) for j in range(nj) for k in range(2))
        z = jnp.zeros((8, 128), f32)

        def tile(i, carry):
            q, m, acc = list(carry[:2 * nj]), list(carry[2 * nj:4 * nj]), list(carry[4 * nj:])
            ii = L // 16 - 1 - i
            for j in range(nj):
                lr_, li_ = lane(128 * j, 128), lane(N + 128 * j, 128)
                p0, p1 = cst[14, :, lr_], cst[15, :, lr_]
                e0, e1 = cst[16, :, lr_], -cst[17, :, lr_]
                cfr, cfi = cst[18, :, lr_], cst[19, :, lr_]
                rr, ri = [None, None], [None, None]
                for h in (1, 0):
                    rows = rows_at(s * L + ii * 16 + 8 * h, 8)
                    vr, vi = cmul(p0, p1, q[2 * j], q[2 * j + 1])
                    ar, ai = mu[rows, lr_] + vr, mu[rows, li_] + vi
                    q[2 * j], q[2 * j + 1] = cmul(q[2 * j], q[2 * j + 1], e0, e1)
                    nr = jnp.where(row1 == 7, m[2 * j], pltpu.roll(ar, 7, 0))
                    ni = jnp.where(row1 == 7, m[2 * j + 1], pltpu.roll(ai, 7, 0))
                    m[2 * j] = jnp.broadcast_to(ar[0:1, :], (8, 128))
                    m[2 * j + 1] = jnp.broadcast_to(ai[0:1, :], (8, 128))
                    xr, xi = st[rows, lr_], st[rows, li_]
                    ur, ui = raw[rows, lr_], raw[rows, li_]
                    acc[4 * j] = acc[4 * j] + nr * xr + ni * xi
                    acc[4 * j + 1] = acc[4 * j + 1] + ni * xr - nr * xi
                    acc[4 * j + 2] = acc[4 * j + 2] + ar * ur + ai * ui
                    acc[4 * j + 3] = acc[4 * j + 3] + ai * ur - ar * ui
                    rr[h] = cfr * ar + cfi * ai
                    ri[h] = cfr * ai - cfi * ar
                rows = rows_at(s * L + ii * 16, 16)
                nb[rows, lr_] = jnp.concatenate(rr, 0).astype(bf16)
                nb[rows, li_] = jnp.concatenate(ri, 0).astype(bf16)
            return tuple(q) + tuple(m) + tuple(acc)

        fin = lax.fori_loop(0, L // 16, tile, q0 + q0 + (z,) * (4 * nj))
        for j in range(nj):
            for k in range(4):
                vv[3 + k:4 + k, 128 * j:128 * j + 128] += jnp.sum(fin[4 * nj + 4 * j + k], 0, keepdims=True)
        rows = pl.ds(s * L, L)
        tmp[rows, :] = nn(nb[rows, :], w4[0:2].reshape(2 * N, H))

        def tok_tile(i, acc):
            for u in range(4):
                rows = rows_at(s * L + i * 128 + u * 32, 32)
                n = tmp[rows, :] + skip_r * pg[rows, :]
                xt = xh[rows, :]
                h = n * gain_r
                m1 = jnp.mean(h, -1, keepdims=True)
                m2 = jnp.mean(h * xt, -1, keepdims=True)
                tgb[rows, :] = ((h - m1 - xt * m2) * rs[rows, 0:1]).astype(bf16)
                acc = acc + fold(n * xt)
            return acc

        accv[2] += lax.fori_loop(0, L // 128, tok_tile, jnp.zeros((8, H), f32))
        there = rows_at(R * t + L * s, L)
        locals_.append(local(tgb.at[rows, tl], tg_hbm.at[there, :]))
        return [remote(tgb.at[rows, lane(U * p[2], U)], tg_hbm.at[there, :], p) for p in zpeer]

    b0 = back_one(0)
    b1 = back_one(1)
    tgc = back_two(0, b0)
    b2 = back_one(2)

    gcf, gbf = gc.reshape(2 * N, H), gb.reshape(2 * N, H)
    ol = lane(HD * (1 - d), HD)

    def gc_step(j, _):
        gcf[rows_at(j * 256, 256), :] = tn(sb[:, lane(j * 256, 256)], plb[...]).astype(bf16)
        return 0

    lax.fori_loop(0, 2 * N // 256, gc_step, 0)
    d1c = remote(gc.at[:, :, :, ol], r1c, sib)

    def gg_step(j, _):
        gg[rows_at(j * 256, 256), :] = tn(act[:, lane(j * 256, 256)], gl[...]).astype(bf16)
        return 0

    lax.fori_loop(0, H // 256, gg_step, 0)
    d1g = remote(gg.at[rows_at(HD * (1 - d), HD), :], r1g, sib)
    tgc += back_two(1, b1)

    def gb_step(j, _):
        gbf[rows_at(j * 256, 256), :] = tn(nb[:, lane(j * 256, 256)], nrm[...]).astype(bf16)
        return 0

    hs = NS // 2

    def rs_ctx(p):
        return p // 2, rows_at(hs * lax.rem(p, 2), hs)

    gr = lambda p: rows_at(uq * p, uq)

    def add2(a, b):
        return (a.astype(f32) + b.astype(f32)).astype(bf16)

    def total(first_, buf, n):
        acc = first_.astype(f32)
        for k in range(n):
            acc = acc + buf[k].astype(f32)
        return acc

    def two_states(g, d1, r1, s1, r2):
        arrived(d1)
        s1[...] = add2(g[:, :, :, dl], r1[...])
        return [remote(s1.at[rs_ctx(p[1])[0], :, rs_ctx(p[1])[1], :], r2.at[k], p) for k, p in enumerate(cpeer)]

    def three_states(d2, s1, r2, s2, r3):
        arrived(*d2)
        s2[...] = total(s1[rs_ctx(c)[0], :, rs_ctx(c)[1], :], r2, C - 1).astype(bf16)
        return [remote(s2.at[t1], r3.at[0], z1), remote(s2.at[t3], r3.at[1], z1)]

    def four_states(d3, s2, r3, s3, r4):
        arrived(*d3)
        s3[0] = add2(s2[t], r3[0])
        s3[1] = add2(s2[t2], r3[1])
        return remote(s3.at[1], r4, z2)

    def five(d4, s3, r4, out):
        arrived(d4)
        out[c] = add2(s3[0], r4[...])
        return [remote(out.at[c], out.at[c], p) for p in cpeer]

    def extra_fix(k):
        incoming(1 + k, fce[1 + k], S, True)
        fix_batch(rawe.at[k], sbe, 1 + k, False)

    def extra_act(k):
        def ssm(rows):
            tmpe[rows, :] = nn(sbe[rows, :], w4[2:4].reshape(2 * N, H))

        each_seq(ssm)

        def gelu(i, rows):
            pre = tmpe[rows, :] + skip_r * nrme[rows_at(R * k + i * 32, 32), :].astype(f32)
            acte[rows, :] = (pre * (0.5 + 0.5 * jnp.tanh(pre * (SQ2PI + (SQ2PI * 0.044715) * (pre * pre))))).astype(bf16)

        tiles(gelu)

    def extra_out(k):
        rank = erank[k]

        def gate(rows):
            tmpe[rows, 0:U] = nn(acte[rows, :], gt[:, tl])

        each_seq(gate)
        bias_u = jnp.sum(jnp.where(lax.broadcasted_iota(jnp.int32, (T, U), 0) == t, bias_t, 0.0), 0, keepdims=True)

        def fin(i, rows):
            here = rows_at(R * k + i * 32, 32)
            sg = logistic(tmpe[rows, 0:U] + bias_u)
            o = valid_of(i, rank) * (xe[here, tl].astype(f32) + acte[rows, tl].astype(f32) * sg)
            obe[here, :] = o.astype(bf16)

        tiles(fin)
        locals_.append(local(obe.at[pl.ds(R * k, R)], out_hbm.at[rows_at(R * rank, R), :]))

    bias_t = jnp.concatenate([bias_r[:, U * k:U * k + U] for k in range(T)], 0)
    d2c = two_states(gc, d1c, r1c, s1c, r2c)
    arrived(d1g)
    s1g[...] = add2(gg[dr_, :], r1g[...])
    d2g = [remote(s1g.at[gr(p[1]), :], r2g.at[k], p) for k, p in enumerate(cpeer)]
    tgc += back_two(2, b2)
    lax.fori_loop(0, 2 * N // 256, gb_step, 0)
    d1b = remote(gb.at[:, :, :, ol], r1b, sib)
    for k, row in ((2, 0), (1, 1), (0, 2)):
        vv[row:row + 1, :] = jnp.sum(accv[k], 0, keepdims=True)
    d1v = remote(vv, vr1, sib)
    extra_fix(0)
    d2b = two_states(gb, d1b, r1b, s1b, r2b)
    arrived(d1v)
    vr2[0] = vv[...] + vr1[...]
    d2v = [remote(vr2.at[0], vr2.at[k + 1], p) for k, p in enumerate(cpeer)]
    extra_start(1)
    extra_act(0)
    extra_out(0)
    d3c = three_states(d2c, s1c, r2c, s2c, r3c)
    arrived(*d2g)
    s2g[...] = total(s1g[gr(c), :], r2g, C - 1).astype(bf16)
    d3g = [remote(s2g.at[:, gl1], r3g.at[0], z1), remote(s2g.at[:, lane(U * t3, U)], r3g.at[1], z1)]
    d3b = three_states(d2b, s1b, r2b, s2b, r3b)
    arrived(*d2v)
    vr3[0] = vr2[0] + vr2[1] + vr2[2] + vr2[3]
    d3v = [remote(vr3.at[0], vr3.at[k + 1], p) for k, p in enumerate(zpeer)]
    extra_fix(1)
    d4c = four_states(d3c, s2c, r3c, s3c, r4c)
    arrived(*d3g)
    s3g[0] = add2(s2g[:, tl], r3g[0])
    s3g[1] = add2(s2g[:, gl2], r3g[1])
    d4g = remote(s3g.at[1], r4g, z2)
    d4b = four_states(d3b, s2b, r3b, s3b, r4b)
    extra_act(1)
    d5 = five(d4c, s3c, r4c, fc_ref) + five(d4g, s3g, r4g, fg_ref) + five(d4b, s3b, r4b, fb_ref)
    extra_out(1)

    arrived(*d3v)
    vf[...] = vr3[0] + vr3[1] + vr3[2] + vr3[3]
    place = t * D + d
    back = lambda n: lax.rem(H - n * place, H)
    st8 = pltpu.roll(vf[...], back(NS // D), 1)[:, 0:NS // D]
    ub8 = pltpu.roll(vf[...], back(U // D), 1)[:, 0:U // D]
    lr1, li1, step1 = lre_in[...], lim_in[...], jnp.exp(stp_in[...])
    dr1, di1, cr1, ci1 = (sm_ref[k:k + 1, 0:NS // D] for k in range(4))
    gdr, gdi, gcr, gci = (st8[k:k + 1] for k in range(3, 7))
    inv = 1.0 / (lr1 * lr1 + li1 * li1)
    hdr = gdr + (gcr * lr1 - gci * li1) * inv
    hdi = gdi + (gcr * li1 + gci * lr1) * inv
    pull = 2.0 * (gcr * cr1 + gci * ci1)
    e1, e2 = dr1 - 1.0, hdr * dr1 + hdi * di1
    e3 = hdi * dr1 - hdr * di1
    fv_ref[...] = jnp.zeros_like(fv_ref)
    fv_ref[0:1, :] = vf[0:1, dl]
    fv_ref[1:2, :] = vf[1:2, dl]
    fv_ref[2:3, 0:U // D] = ub8[2:3]
    fv_ref[3:4, 0:NS // D] = (gcr * e1 + gci * di1 - pull * lr1) * inv + step1 * e2
    fv_ref[4:5, 0:NS // D] = (gcr * di1 - gci * e1 - pull * li1) * inv + step1 * e3
    fv_ref[5:6, 0:NS // D] = step1 * (lr1 * e2 + li1 * e3)
    arrived(*d5, *tgc, *outc)
    for cp in locals_:
        cp.wait()
    for cp in started:
        cp.wait_send()
    assert count[0] == NSEM and nlocal[0] == NLOCAL, (count[0], nlocal[0])


NSEM, NLOCAL = 117, 21


def fused_call(geo, lens, x2, og2, *params):
    D, C, T, S, L, H, N, U = geo
    R, NS, HD = S * L, N // T, H // D
    f32, bf16 = jnp.float32, jnp.bfloat16
    uq, hs = HD // C, NS // 2
    V = pltpu.VMEM
    any_, vm = pl.BlockSpec(memory_space=pl.ANY), pl.BlockSpec(memory_space=pltpu.VMEM)
    scratch = [
        V((R, H), bf16), V((R, H), bf16), V((R, H), f32), V((R, 128), f32),
        V((R, 2 * N), f32), V((R, 2 * N), f32), V((R, 2 * N), bf16),
        V((R, H), f32), V((R, H), bf16), V((R, H), f32), V((R, H), f32),
        V((R, H), bf16), V((R, H), bf16), V((R, H), bf16), V((R, H), f32), V((R, H), bf16),
        V((R, 2 * N), f32), V((R, 2 * N), bf16), V((R, H), bf16),
        V((2 * R, H), bf16), V((2 * R, H), bf16), V((2, R, 2 * N), f32), V((R, 2 * N), bf16),
        V((R, H), bf16), V((R, H), f32), V((2 * R, U), bf16),
        V((4, T, NS, H), bf16), V((H, H), bf16), V((D * T, 8, HD), f32),
        V((22, 8, N), f32), V((6, 8, N), f32), V((6, C - 1, 8, N), f32), V((6, 8, N), f32),
        V((2, T, NS, H), bf16), V((H, H), bf16), V((2, T, NS, H), bf16),
        V((2, T, NS, HD), bf16), V((HD, H), bf16), V((2, T, NS, HD), bf16),
        V((2, T, NS, HD), bf16), V((HD, H), bf16), V((2, T, NS, HD), bf16),
        V((C - 1, T, hs, HD), bf16), V((C - 1, uq, H), bf16), V((C - 1, T, hs, HD), bf16),
        V((T, hs, HD), bf16), V((uq, H), bf16), V((T, hs, HD), bf16),
        V((2, hs, HD), bf16), V((2, uq, U), bf16), V((2, hs, HD), bf16),
        V((2, hs, HD), bf16), V((2, uq, U), bf16), V((2, hs, HD), bf16),
        V((hs, HD), bf16), V((uq, U), bf16), V((hs, HD), bf16),
        V((8, H), f32), V((8, H), f32), V((C, 8, H), f32), V((T, 8, H), f32), V((8, H), f32), V((3, 8, H), f32),
        V((4, NS, HD), bf16), V((8, HD), f32), V((HD, U), bf16), V((1, HD), f32), V((1, HD), f32),
        V((1, NS // D), f32), V((1, NS // D), f32), V((1, NS // D), f32), V((1, U // D), f32),
        pltpu.SemaphoreType.DMA((NLOCAL,)), pltpu.SemaphoreType.DMA((NSEM,)), pltpu.SemaphoreType.DMA((NSEM,)),
    ]
    rows = x2.shape[0]
    return pl.pallas_call(
        functools.partial(fused_body, geo),
        out_shape=(
            jax.ShapeDtypeStruct((rows, U), bf16), jax.ShapeDtypeStruct((rows, U), bf16),
            jax.ShapeDtypeStruct((C, hs, HD), bf16), jax.ShapeDtypeStruct((C, uq, U), bf16),
            jax.ShapeDtypeStruct((C, hs, HD), bf16), jax.ShapeDtypeStruct((8, HD), f32)),
        in_specs=[pl.BlockSpec(memory_space=pltpu.SMEM), any_, any_] + [any_] * 11,
        out_specs=(any_, any_, vm, vm, vm, vm),
        scratch_shapes=scratch,
        compiler_params=pltpu.CompilerParams(
            collective_id=0, has_side_effects=True, vmem_limit_bytes=60 * 1024 * 1024),
        name="block",
    )(lens, x2, og2, *params)


def finish_body(geo, len_ref, out_in, tok_in, og_in, fc_in, fg_in, fb_in, fv, out, ingrad, gain_g, skip_g,
                lre_g, lim_g, step_g, bre_g, bim_g, cre_g, cim_g, glu_g, bias_g,
                tokv, ogv, outv, fc, fg, fb, bre, bim, cre, cim, glu, res, sem, gsem, osem):
    D, C, T, S, L, H, N, U = geo
    NS = N // T
    f32 = jnp.float32

    def move(src, dst, s):
        cp = pltpu.make_async_copy(src, dst, s)
        cp.start()
        return cp

    part = [pl.ds(S * k, S) for k in range(T)]
    loads = [(move(tok_in.at[part[k]], tokv.at[part[k]], sem.at[0, k]),
              move(og_in.at[part[k]], ogv.at[part[k]], sem.at[1, k])) for k in range(T)]
    params = [move(a, b, gsem.at[k]) for k, (a, b) in enumerate(((fc_in, fc), (fg_in, fg), (fb_in, fb)))]
    passes = [move(out_in.at[part[k]], outv.at[part[k]], sem.at[2, k]) for k in range(T)]
    base = lax.axis_index("ctx") * L
    stores = []
    for k in range(T):
        for cp in loads[k]:
            cp.wait()

        def tile(i, _):
            s = S * k + i // (L // 32)
            r0 = lax.rem(i, L // 32) * 32
            rows = pl.ds(pl.multiple_of(r0, 32), 32)
            pos = base + r0 + lax.broadcasted_iota(jnp.int32, (32, 1), 0)
            keep = jnp.where(pos < len_ref[s], 1.0, 0.0)
            res[s, rows, :] = keep * ogv[s, rows, :].astype(f32) + tokv[s, rows, :].astype(f32)
            return 0

        lax.fori_loop(0, S * L // 32, tile, 0)
        stores.append(move(res.at[part[k]], ingrad.at[part[k]], osem.at[k]))
    for cp in params:
        cp.wait()
    h = C // 2
    for k in range(C):
        rows = pl.ds((k % h) * (NS // h), NS // h)
        (bre if k < h else bim)[rows, :] = fb[k].astype(f32)
        (cre if k < h else cim)[rows, :] = fc[k].astype(f32)
    glu[...] = fg[...].reshape(glu.shape).astype(f32)
    pairs = ((bre, bre_g), (bim, bim_g), (cre, cre_g), (cim, cim_g), (glu, glu_g))
    stores += [move(a, b, osem.at[2 * T + k]) for k, (a, b) in enumerate(pairs)]
    for k in range(T):
        passes[k].wait()
        stores.append(move(outv.at[part[k]], out.at[part[k]], osem.at[T + k]))
    gain_g[...] = fv[0:1, :]
    skip_g[...] = fv[1:2, :]
    bias_g[...] = fv[2:3, 0:U // D]
    lre_g[...] = fv[3:4, 0:NS // D]
    lim_g[...] = fv[4:5, 0:NS // D]
    step_g[...] = fv[5:6, 0:NS // D]
    for cp in stores:
        cp.wait()


def finish_call(geo, lens, out, tok, og, fc, fg, fb, fv):
    D, C, T, S, L, H, N, U = geo
    NS, HD = N // T, H // D
    f32, bf16 = jnp.float32, jnp.bfloat16
    seqs = S * T
    any_, vm = pl.BlockSpec(memory_space=pl.ANY), pl.BlockSpec(memory_space=pltpu.VMEM)
    V = pltpu.VMEM
    small = [(1, HD), (1, HD)] + [(1, NS // D)] * 3 + [(NS, HD)] * 4 + [(HD, U), (1, U // D)]
    return pl.pallas_call(
        functools.partial(finish_body, geo),
        out_shape=[jax.ShapeDtypeStruct((seqs, L, U), bf16), jax.ShapeDtypeStruct((seqs, L, U), f32)]
        + [jax.ShapeDtypeStruct(s, f32) for s in small],
        in_specs=[pl.BlockSpec(memory_space=pltpu.SMEM)] + [any_] * 6 + [vm],
        out_specs=[any_, any_] + [vm] * 5 + [any_] * 5 + [vm],
        scratch_shapes=[V((seqs, L, U), bf16)] * 3 + [V(a.shape, a.dtype) for a in (fc, fg, fb)]
        + [V((NS, HD), f32)] * 4 + [V((HD, U), f32), V((seqs, L, U), f32)]
        + [pltpu.SemaphoreType.DMA((3, T)), pltpu.SemaphoreType.DMA((3,)), pltpu.SemaphoreType.DMA((2 * T + 5,))],
        compiler_params=pltpu.CompilerParams(vmem_limit_bytes=60 * 1024 * 1024),
        name="finish",
    )(lens, out.reshape(seqs, L, U), tok.reshape(seqs, L, U), og, fc, fg, fb, fv)


def coefficients(lam_re, lam_im, step_log):
    step = jnp.exp(step_log)
    magnitude = jnp.exp(lam_re * step)
    decay_re = magnitude * jnp.cos(lam_im * step)
    decay_im = magnitude * jnp.sin(lam_im * step)
    inv = 1.0 / (lam_re * lam_re + lam_im * lam_im)
    coef_re = ((decay_re - 1.0) * lam_re + decay_im * lam_im) * inv
    coef_im = (decay_im * lam_re - (decay_re - 1.0) * lam_im) * inv
    return decay_re, decay_im, coef_re, coef_im


def token_split(sizes, inputs, lengths, norm_gain, skip_weight, lambda_re, lambda_im, log_step,
                b_re, b_im, c_re, c_im, glu_weight, glu_bias, out_grad):
    D, C, T = sizes
    seqs, L, H = inputs.shape
    NS, HD = b_re.shape
    U = glu_weight.shape[1]
    geo = (D, C, T, seqs // T, L, H, NS * T, U)
    row = lambda v: v.reshape(1, -1)
    out, tok, fc, fg, fb, fv = fused_call(
        geo, lengths, inputs.reshape(seqs * L, H), out_grad.reshape(seqs * L, U),
        b_re, b_im, c_re.T, c_im.T, glu_weight,
        *(row(v) for v in (norm_gain, skip_weight, lambda_re, lambda_im, log_step, glu_bias)))
    res = finish_call(geo, lengths, out, tok, out_grad, fc, fg, fb, fv)
    out, ingrad, gain_g, skip_g, lre_g, lim_g, step_g, bre_g, bim_g, cre_g, cim_g, glu_g, bias_g = res
    flat = lambda v: v.reshape(-1)
    return (out, ingrad, flat(gain_g), flat(skip_g), flat(lre_g), flat(lim_g), flat(step_g),
            bre_g, bim_g, cre_g.T, cim_g.T, glu_g, flat(bias_g))


def solution(mesh):
    in_specs = (
        P("dp", "ctx", None),
        P("dp"),
        P("dp"),
        P("dp"),
        P(("tp", "dp")),
        P(("tp", "dp")),
        P(("tp", "dp")),
        P("tp", "dp"),
        P("tp", "dp"),
        P("dp", "tp"),
        P("dp", "tp"),
        P("dp", "tp"),
        P(("tp", "dp")),
        P("dp", "ctx", "tp"),
    )
    out_specs = (
        P("dp", "ctx", "tp"),
        P("dp", "ctx", "tp"),
        P("dp"),
        P("dp"),
        P(("tp", "dp")),
        P(("tp", "dp")),
        P(("tp", "dp")),
        P("tp", "dp"),
        P("tp", "dp"),
        P("dp", "tp"),
        P("dp", "tp"),
        P("dp", "tp"),
        P(("tp", "dp")),
    )
    sizes = tuple(mesh.shape[name] for name in ("dp", "ctx", "tp"))

    def block(*args):
        seqs, _, feat = args[0].shape
        units = args[11].shape[1]
        if sizes == (2, 4, 4) and seqs % sizes[2] == 0 and units % 128 == 0:
            return token_split(sizes, *args)
        return on_device(*args)

    return jax.shard_map(
        block, mesh=mesh, in_specs=in_specs, out_specs=out_specs, check_vma=False
    )
```

profile of v0, /device:TPU:0, one launch (start us, length us, event | category | flops | bytes accessed | tf_op | source)
XLA Modules:
  0.0 79.7 jit_solution(6613651230548852021)
XLA Ops:
  0.6 73.8 %block.1 = (bf16[3072,128]{1,0:T(8,128)(2,1)}, bf16[3072,128]{1,0:T(8,128)(2,1)}, bf16[4,48,256]{2,1,0:T(8,128)(2,1)}, bf16[4,64,128]{2,1,0:T(8,128)(2,1)}, bf16...) custom-call(s32[12]{0:T(128)} %len_ref.1, bf16[3072,512]{1,0:T(8,128)(2,1)} %bitcast.20, bf16[3072,128]{1,0:T(8,128)(2,1)} %bitcast.21, ...), custom_call_target="tpu_custom_call" | custom-call | tf_op jit(solution)/shard_map/block/pallas_call | solution.py:1026
  74.5 5.3 %finish.1 = (bf16[12,256,128]{2,1,0:T(8,128)(2,1)}, f32[12,256,128]{2,1,0:T(8,128)}, f32[1,256]{1,0:T(1,128)}, f32[1,256]{1,0:T(1,128)}, f32[1,48]{1,0:T(1,128)}...) custom-call(s32[12]{0:T(128)} %len_ref.1, ...), custom_call_target="tpu_custom_call" | custom-call | tf_op jit(solution)/shard_map/finish/pallas_call | solution.py:1106
where the time goes:
time: 80 us; the launch traced here: 79.7 us
  Pallas kernels  79.1 us (99%)
    pallas_call x1, Pallas kernels, fused_call(): pl.pallas_call(functools.partial(fused_body, geo), out_shape=(jax.ShapeDt...  73.8 us
    pallas_call x1, Pallas kernels, finish_call(): pl.pallas_call(functools.partial(finish_body, geo), out_shape=[jax.ShapeD...  5.28 us

commit v1 on v0

--- a/solution.py
+++ b/solution.py
@@ -330,7 +330,7 @@
     (xv, nrm, xh, rs, raw, st, sb, tmp, act, gp, sig, ogv, ob, gl, pg, plb, mu, nb, tgb,
      xe, nrme, rawe, sbe, acte, tmpe, obe,
      w4, gt, smr, cst, ce, cer, cin, gc, gg, gb, r1c, r1g, r1b, s1c, s1g, s1b, r2c, r2g, r2b,
-     s2c, s2g, s2b, r3c, r3g, r3b, s3c, s3g, s3b, r4c, r4g, r4b,
+     s2c, s2g, s2b, r3c, r3g, r3b, s3c, s3g, r4c, r4g,
      vv, vr1, vr2, vr3, vf, accv, pk, sm_ref, glu, gain_in, skip_in, lre_in, lim_in, stp_in, bias_in,
      lsem, ssem, rsem) = refs[20:]
     d, c, t = lax.axis_index("dp"), lax.axis_index("ctx"), lax.axis_index("tp")
@@ -344,7 +344,7 @@
     sib = (1 - d, c, t)
     xpeer = [(1 - d, c, lax.rem(t + k, T)) for k in range(1, T)]
     everyone = zpeer + cpeer + [sib] + xpeer
-    erank = [t2, t3]
+    erank = [t2]
 
     count = [0]
     started = []
@@ -432,28 +432,22 @@
     pair = rows_at(2 - 2 * half, 2)
     pairl = lane(2 * U * (1 - half), 2 * U)
 
-    def first(k):
-        q = 2 * k + gq
-        return [remote(pk.at[q, :, ql], w4.at[q, t, :, wl], p) for p in (z1, z2)]
-
+    qb, qc = gq, 2 + gq
+    far_b = [remote(pk.at[qb, :, ql], w4.at[qb, t, :, wl], p) for p in (z3, z2)]
     small = [remote(sm_ref, smr.at[me8], p) for p in zpeer + [sib] + xpeer]
-    w1b = first(0)
+    near_b = remote(pk.at[0:2], w4.at[0:2, t, :, dl], z1)
     w3b = [remote(pk.at[0:2], w4.at[0:2, t, :, dl], sib)]
-
-    def pass_on(cp, blk):
-        arrived(cp)
-        return remote(blk, blk, z1)
 
     def spread(blk, *cps):
         arrived(*cps)
         return [remote(blk, blk, p) for p in cpeer]
 
-    qb, qc = gq, 2 + gq
     gl1, gl2 = lane(U * t1, U), lane(U * t2, U)
-    w1b3 = pass_on(w1b[1], w4.at[qb, t2, :, wl])
-    w2b = [spread(w4.at[qb, t1, :, wl], w1b[0])]
-    w1c = first(1)
-    w1g = [remote(glu.at[gown], gt.at[grow, tl], p) for p in (z1, z2)]
+    w2b = spread(w4.at[qb, pair, :, wl], *far_b)
+    far_c = [remote(pk.at[qc, :, ql], w4.at[qc, t, :, wl], p) for p in (z3, z2)]
+    far_g = [remote(glu.at[gown], gt.at[grow, tl], p) for p in (z3, z2)]
+    near_c = remote(pk.at[2:4], w4.at[2:4, t, :, dl], z1)
+    near_g = remote(glu, gt.at[dr_, tl], z1)
     w3c = [remote(pk.at[2:4], w4.at[2:4, t, :, dl], sib)]
     w3g = [remote(glu, gt.at[dr_, tl], sib)]
 
@@ -473,7 +467,8 @@
     both = jnp.concatenate([smr[t], smr[T + t]], 1)
     gain_r, skip_r, bias_r = both[5:6, :], both[6:7, :], bias[4:5, :]
 
-    w2b.append(spread(w4.at[qb, pair, :, wl], w1b3))
+    arrived(near_b)
+    w3b.append(remote(w4.at[0:2, t1, :, dl], w4.at[0:2, t1, :, dl], sib))
     row8 = lax.broadcasted_iota(jnp.int32, (8, N), 0)
     full = lambda v, k, n: jnp.broadcast_to(v[k:k + 1, :n], (8, n))
     dr, di = full(vec, 0, N), full(vec, 1, N)
@@ -510,10 +505,6 @@
         return 0
 
     lax.fori_loop(0, R // 32, nrm_tile, 0)
-    w1c3 = pass_on(w1c[1], w4.at[qc, t2, :, wl])
-    w2c = [spread(w4.at[qc, t1, :, wl], w1c[0])]
-    w1g3 = pass_on(w1g[1], gt.at[grow, gl2])
-    w2g = [spread(gt.at[grow, gl1], w1g[0])]
     og = [cot_send(0)]
 
     def lne_tile(i, _):
@@ -522,28 +513,16 @@
             nrme[rows, :] = (standard(xe[rows, :].astype(f32))[0] * gain_r).astype(bf16)
         return 0
 
-    for cp in cxe:
-        cp.wait()
-    lax.fori_loop(0, R // 128, lne_tile, 0)
-    w2c.append(spread(w4.at[qc, pair, :, wl], w1c3))
-    w2g.append(spread(gt.at[grow, pairl], w1g3))
-    og.append(cot_send(1))
-    arrived(*w2b[0])
-    w3b.append(remote(w4.at[0:2, t1, :, dl], w4.at[0:2, t1, :, dl], sib))
-    og.append(cot_send(2))
-    lax.fori_loop(R // 128, 2 * R // 128, lne_tile, 0)
-    arrived(*w2b[1])
-    w3b.append(remote(w4.at[0:2, pair, :, dl], w4.at[0:2, pair, :, dl], sib))
-
     def seq_rows(s):
         return rows_at(s * L, L)
 
-    def drive(src, dst, lo, hi, off):
-        def step(s, _):
-            dst[seq_rows(s), :] = nt(src[seq_rows(s + off), :], w4[0:2].reshape(2 * N, H))
-            return 0
-
-        lax.fori_loop(lo, hi, step, 0)
+    wv = w4.reshape(4, N, H)
+
+    def drive(src, off, dst, j):
+        rows = rows_at(128 * j, 128)
+        both_ = nt(src[pl.ds(off, R), :], jnp.concatenate([wv[0, rows, :], wv[1, rows, :]], 0))
+        dst[:, lane(128 * j, 128)] = both_[:, 0:128]
+        dst[:, lane(N + 128 * j, 128)] = both_[:, 128:256]
 
     def scan(src, dst, groups, base, coef, reverse):
         e = 0 if reverse else 7
@@ -584,15 +563,20 @@
         z = jnp.zeros((8, 128), f32)
         return lax.fori_loop(0, L // 32, tile, (z,) * (2 * len(groups)))
 
-    def scan_batch(src, dst, slot):
-        def lanes_step(j, _):
-            fin = scan(src, dst, [(s * L, 128 * j) for s in range(S)], 0, True, False)
-            for s in range(S):
-                ce[slot, pl.ds(s, 1), lane(128 * j, 128)] = fin[2 * s][0:1, :]
-                ce[slot, pl.ds(S + s, 1), lane(128 * j, 128)] = fin[2 * s + 1][0:1, :]
+    def begin(src, off, dst, out, slot, j):
+        drive(src, off, dst, j)
+        fin = scan(dst, out, [(s * L, 128 * j) for s in range(S)], 0, True, False)
+        for s in range(S):
+            ce[slot, pl.ds(s, 1), lane(128 * j, 128)] = fin[2 * s][0:1, :]
+            ce[slot, pl.ds(S + s, 1), lane(128 * j, 128)] = fin[2 * s + 1][0:1, :]
+
+    def rest(*what):
+        def step(k, _):
+            begin(*what, 1 + k * (1 - 2 * half))
             return 0
 
-        lax.fori_loop(0, N // 128, lanes_step, 0)
+        lax.fori_loop(0, 2, step, 0)
+        slot = what[4 - 0]
         return [remote(ce.at[slot], cer.at[slot, k], p) for k, p in enumerate(cpeer)]
 
     def incoming(slot, cps, n, forward):
@@ -648,11 +632,7 @@
         lax.fori_loop(0, N // 128, fix_lanes, 0)
 
     def each_seq(f):
-        def step(s, _):
-            f(seq_rows(s))
-            return 0
-
-        lax.fori_loop(0, S, step, 0)
+        f(pl.ds(0, R))
 
     def tiles(f, lo=0, hi=R // 32):
         def step(i, _):
@@ -669,24 +649,35 @@
     def logistic(v):
         return 0.5 + 0.5 * jnp.tanh(0.5 * v)
 
+    batches = [(nrm, 0, raw, st, 0)] + [(nrme, R * k, rawe.at[k], rawe.at[k], 1 + k) for k in range(len(erank))]
     arrived(*w3b)
-    drive(nrm, raw, 0, S, 0)
-    fce = [scan_batch(raw, st, 0)]
-    arrived(*w2c[0])
+    begin(*batches[0], 2 * half)
+    w2c = spread(w4.at[qc, pair, :, wl], *far_c)
+    w2g = spread(gt.at[grow, pairl], *far_g)
+    og.append(cot_send(1))
+    for cp in cxe:
+        cp.wait()
+    lax.fori_loop(0, R // 128, lne_tile, 0)
+    arrived(*w2b)
+    w3b2 = remote(w4.at[0:2, pair, :, dl], w4.at[0:2, pair, :, dl], sib)
+    og.append(cot_send(2))
+    begin(*batches[1], 2 * half)
+    arrived(w3b2)
+    fce = [rest(*batches[0])]
+    arrived(near_c)
     w3c.append(remote(w4.at[2:4, t1, :, dl], w4.at[2:4, t1, :, dl], sib))
-    arrived(*w2c[1])
+    arrived(near_g)
+    blk = gt.at[dr_, gl1]
+    w3g.append(remote(blk, blk, sib))
+    arrived(*w2c)
     w3c.append(remote(w4.at[2:4, pair, :, dl], w4.at[2:4, pair, :, dl], sib))
-    arrived(*w2g[0], *w2g[1])
-    blk = gt.at[dr_, lane(U * t1, U)]
-    w3g.append(remote(blk, blk, sib))
+    arrived(*w2g)
     blk = gt.at[dr_, pairl]
     w3g.append(remote(blk, blk, sib))
-
-    def extra_start(k):
-        drive(nrme, rawe.at[k], 0, S, S * k)
-        fce.append(scan_batch(rawe.at[k], rawe.at[k], 1 + k))
-
-    extra_start(0)
+    fce.append(rest(*batches[1]))
+    if len(erank) > 1:
+        lax.fori_loop(R // 128, 2 * R // 128, lne_tile, 0)
+        begin(*batches[2], 2 * half)
     incoming(0, fce[0], S, True)
     fix_batch(st, sb, 0, True)
     arrived(*w3c)
@@ -719,7 +710,7 @@
         ob[rows, :] = o.astype(bf16)
 
     tiles(out_tile)
-    outc = [remote(ob.at[:, lane(U * t1, U)], out_hbm.at[mine, :], z1)]
+    outc = [remote(ob.at[:, lane(U * q, U)], out_hbm.at[mine, :], p) for q, p in ((t1, z1), (t3, z3))]
     locals_ = [local(ob.at[:, tl], out_hbm.at[mine, :])]
 
     def fold(v):
@@ -823,10 +814,7 @@
         locals_.append(local(tgb.at[rows, tl], tg_hbm.at[there, :]))
         return [remote(tgb.at[rows, lane(U * p[2], U)], tg_hbm.at[there, :], p) for p in zpeer]
 
-    b0 = back_one(0)
-    b1 = back_one(1)
-    tgc = back_two(0, b0)
-    b2 = back_one(2)
+    bs = [back_one(s) for s in range(S)]
 
     gcf, gbf = gc.reshape(2 * N, H), gb.reshape(2 * N, H)
     ol = lane(HD * (1 - d), HD)
@@ -844,7 +832,6 @@
 
     lax.fori_loop(0, H // 256, gg_step, 0)
     d1g = remote(gg.at[rows_at(HD * (1 - d), HD), :], r1g, sib)
-    tgc += back_two(1, b1)
 
     def gb_step(j, _):
         gbf[rows_at(j * 256, 256), :] = tn(nb[:, lane(j * 256, 256)], nrm[...]).astype(bf16)
@@ -922,42 +909,55 @@
         locals_.append(local(obe.at[pl.ds(R * k, R)], out_hbm.at[rows_at(R * rank, R), :]))
 
     bias_t = jnp.concatenate([bias_r[:, U * k:U * k + U] for k in range(T)], 0)
+    tgc = back_two(0, bs[0])
     d2c = two_states(gc, d1c, r1c, s1c, r2c)
     arrived(d1g)
     s1g[...] = add2(gg[dr_, :], r1g[...])
     d2g = [remote(s1g.at[gr(p[1]), :], r2g.at[k], p) for k, p in enumerate(cpeer)]
-    tgc += back_two(2, b2)
+    for k in range(1, S):
+        tgc += back_two(k, bs[k])
     lax.fori_loop(0, 2 * N // 256, gb_step, 0)
     d1b = remote(gb.at[:, :, :, ol], r1b, sib)
     for k, row in ((2, 0), (1, 1), (0, 2)):
         vv[row:row + 1, :] = jnp.sum(accv[k], 0, keepdims=True)
     d1v = remote(vv, vr1, sib)
-    extra_fix(0)
+    if erank:
+        extra_fix(0)
     d2b = two_states(gb, d1b, r1b, s1b, r2b)
     arrived(d1v)
     vr2[0] = vv[...] + vr1[...]
     d2v = [remote(vr2.at[0], vr2.at[k + 1], p) for k, p in enumerate(cpeer)]
-    extra_start(1)
-    extra_act(0)
-    extra_out(0)
+    if len(erank) > 1:
+        fce.append(rest(*batches[2]))
     d3c = three_states(d2c, s1c, r2c, s2c, r3c)
     arrived(*d2g)
     s2g[...] = total(s1g[gr(c), :], r2g, C - 1).astype(bf16)
     d3g = [remote(s2g.at[:, gl1], r3g.at[0], z1), remote(s2g.at[:, lane(U * t3, U)], r3g.at[1], z1)]
-    d3b = three_states(d2b, s1b, r2b, s2b, r3b)
-    arrived(*d2v)
-    vr3[0] = vr2[0] + vr2[1] + vr2[2] + vr2[3]
-    d3v = [remote(vr3.at[0], vr3.at[k + 1], p) for k, p in enumerate(zpeer)]
-    extra_fix(1)
+    if erank:
+        extra_act(0)
     d4c = four_states(d3c, s2c, r3c, s3c, r4c)
     arrived(*d3g)
     s3g[0] = add2(s2g[:, tl], r3g[0])
     s3g[1] = add2(s2g[:, gl2], r3g[1])
     d4g = remote(s3g.at[1], r4g, z2)
-    d4b = four_states(d3b, s2b, r3b, s3b, r4b)
-    extra_act(1)
-    d5 = five(d4c, s3c, r4c, fc_ref) + five(d4g, s3g, r4g, fg_ref) + five(d4b, s3b, r4b, fb_ref)
-    extra_out(1)
+    if erank:
+        extra_out(0)
+    arrived(*d2b)
+    s2b[...] = total(s1b[rs_ctx(c)[0], :, rs_ctx(c)[1], :], r2b, C - 1).astype(bf16)
+    d3b = [remote(s2b.at[p[2]], r3b.at[k], p) for k, p in enumerate(zpeer)]
+    arrived(*d2v)
+    vr3[0] = vr2[0] + vr2[1] + vr2[2] + vr2[3]
+    d3v = [remote(vr3.at[0], vr3.at[k + 1], p) for k, p in enumerate(zpeer)]
+    if len(erank) > 1:
+        extra_fix(1)
+    d5 = five(d4c, s3c, r4c, fc_ref) + five(d4g, s3g, r4g, fg_ref)
+    if len(erank) > 1:
+        extra_act(1)
+    arrived(*d3b)
+    fb_ref[c] = total(s2b[t], r3b, T - 1).astype(bf16)
+    d5 += [remote(fb_ref.at[c], fb_ref.at[c], p) for p in cpeer]
+    if len(erank) > 1:
+        extra_out(1)
 
     arrived(*d3v)
     vf[...] = vr3[0] + vr3[1] + vr3[2] + vr3[3]
@@ -989,7 +989,7 @@
     assert count[0] == NSEM and nlocal[0] == NLOCAL, (count[0], nlocal[0])
 
 
-NSEM, NLOCAL = 117, 21
+NSEM, NLOCAL = 106, 19
 
 
 def fused_call(geo, lens, x2, og2, *params):
@@ -1014,9 +1014,8 @@
         V((2, T, NS, HD), bf16), V((HD, H), bf16), V((2, T, NS, HD), bf16),
         V((C - 1, T, hs, HD), bf16), V((C - 1, uq, H), bf16), V((C - 1, T, hs, HD), bf16),
         V((T, hs, HD), bf16), V((uq, H), bf16), V((T, hs, HD), bf16),
-        V((2, hs, HD), bf16), V((2, uq, U), bf16), V((2, hs, HD), bf16),
-        V((2, hs, HD), bf16), V((2, uq, U), bf16), V((2, hs, HD), bf16),
-        V((hs, HD), bf16), V((uq, U), bf16), V((hs, HD), bf16),
+        V((2, hs, HD), bf16), V((2, uq, U), bf16), V((T - 1, hs, HD), bf16),
+        V((2, hs, HD), bf16), V((2, uq, U), bf16), V((hs, HD), bf16), V((uq, U), bf16),
         V((8, H), f32), V((8, H), f32), V((C, 8, H), f32), V((T, 8, H), f32), V((8, H), f32), V((3, 8, H), f32),
         V((4, NS, HD), bf16), V((8, HD), f32), V((HD, U), bf16), V((1, HD), f32), V((1, HD), f32),
         V((1, NS // D), f32), V((1, NS // D), f32), V((1, NS // D), f32), V((1, U // D), f32),

time: 80 us -> 75.6 us (0.945)
  Pallas kernels: 79.1 us -> 74.7 us
    pallas_call x1, Pallas kernels: 73.8 us -> 69.4 us  [fused_call(): pl.pallas_call(functools.partial(fused_body, geo), out_shape=(jax.ShapeDt...]
where the time goes in v1:
time: 75.6 us; the launch traced here: 75.4 us
  Pallas kernels  74.7 us (99%)
    pallas_call x1, Pallas kernels, fused_call(): pl.pallas_call(functools.partial(fused_body, geo), out_shape=(jax.ShapeDt...  69.4 us
    pallas_call x1, Pallas kernels, finish_call(): pl.pallas_call(functools.partial(finish_body, geo), out_shape=[jax.ShapeD...  5.28 us

profile of v1, /device:TPU:0, one launch (start us, length us, event | category | flops | bytes accessed | tf_op | source)
XLA Modules:
  0.0 75.4 jit_solution(9023177535123863243)
XLA Ops:
  0.6 69.4 %block.1 = (bf16[3072,128]{1,0:T(8,128)(2,1)}, bf16[3072,128]{1,0:T(8,128)(2,1)}, bf16[4,48,256]{2,1,0:T(8,128)(2,1)}, bf16[4,64,128]{2,1,0:T(8,128)(2,1)}, bf16...) custom-call(s32[12]{0:T(128)} %len_ref.1, bf16[3072,512]{1,0:T(8,128)(2,1)} %bitcast.20, bf16[3072,128]{1,0:T(8,128)(2,1)} %bitcast.21, ...), custom_call_target="tpu_custom_call" | custom-call | tf_op jit(solution)/shard_map/block/pallas_call | solution.py:1025
  70.1 5.3 %finish.1 = (bf16[12,256,128]{2,1,0:T(8,128)(2,1)}, f32[12,256,128]{2,1,0:T(8,128)}, f32[1,256]{1,0:T(1,128)}, f32[1,256]{1,0:T(1,128)}, f32[1,48]{1,0:T(1,128)}...) custom-call(s32[12]{0:T(128)} %len_ref.1, ...), custom_call_target="tpu_custom_call" | custom-call | tf_op jit(solution)/shard_map/finish/pallas_call | solution.py:1105

commit v2 on v1

--- a/solution.py
+++ b/solution.py
@@ -319,19 +319,19 @@
     return pl.ds(pl.multiple_of(start, 128), size)
 
 
-def fused_body(geo, *refs):
+def fused_body(geo, extra, *refs):
     D, C, T, S, L, H, N, U = geo
     R = S * L
     NS = N // T
     HD = H // D
     f32, bf16 = jnp.float32, jnp.bfloat16
     (len_ref, x_hbm, og_hbm, bre, bim, cre, cim, glu_hbm, gain_h, skip_h, lre_h, lim_h, stp_h, bias_h,
-     out_hbm, tg_hbm, fc_ref, fg_ref, fb_ref, fv_ref) = refs[:20]
+     out_hbm, tg_hbm, fc_hbm, fg_hbm, fb_hbm, fv_hbm) = refs[:20]
     (xv, nrm, xh, rs, raw, st, sb, tmp, act, gp, sig, ogv, ob, gl, pg, plb, mu, nb, tgb,
      xe, nrme, rawe, sbe, acte, tmpe, obe,
      w4, gt, smr, cst, ce, cer, cin, gc, gg, gb, r1c, r1g, r1b, s1c, s1g, s1b, r2c, r2g, r2b,
      s2c, s2g, s2b, r3c, r3g, r3b, s3c, s3g, r4c, r4g,
-     vv, vr1, vr2, vr3, vf, accv, pk, sm_ref, glu, gain_in, skip_in, lre_in, lim_in, stp_in, bias_in,
+     q5c, q5g, q5b, vv, vr1, vr2, vr3, accv, pk, sm_ref, glu, gain_in, skip_in, lre_in, lim_in, stp_in, bias_in,
      lsem, ssem, rsem) = refs[20:]
     d, c, t = lax.axis_index("dp"), lax.axis_index("ctx"), lax.axis_index("tp")
     half = t // 2
@@ -344,7 +344,8 @@
     sib = (1 - d, c, t)
     xpeer = [(1 - d, c, lax.rem(t + k, T)) for k in range(1, T)]
     everyone = zpeer + cpeer + [sib] + xpeer
-    erank = [t2]
+    erank = [t2, t3][:len(extra)]
+    eoff = [L * sum(extra[:k]) for k in range(len(extra))]
 
     count = [0]
     started = []
@@ -382,7 +383,8 @@
     mine = rows_at(R * t, R)
     cp_pk = [local(a, pk.at[k]) for k, a in enumerate((bre, bim, cre, cim))] + [local(glu_hbm, glu)]
     cx = local(x_hbm.at[mine], xv)
-    cxe = [local(x_hbm.at[rows_at(R * e, R)], xe.at[pl.ds(R * k, R)]) for k, e in enumerate(erank)]
+    cxe = [local(x_hbm.at[pl.ds(pl.multiple_of(R * e, R), L * n)], xe.at[pl.ds(o, L * n)])
+           for e, n, o in zip(erank, extra, eoff)]
     co = local(og_hbm.at[mine], ogv.at[:, lane(U * t, U)])
     dl = lane(HD * d, HD)
     dr_ = rows_at(HD * d, HD)
@@ -518,11 +520,11 @@
 
     wv = w4.reshape(4, N, H)
 
-    def drive(src, off, dst, j):
+    def drive(src, off, dst, n, j):
         rows = rows_at(128 * j, 128)
-        both_ = nt(src[pl.ds(off, R), :], jnp.concatenate([wv[0, rows, :], wv[1, rows, :]], 0))
-        dst[:, lane(128 * j, 128)] = both_[:, 0:128]
-        dst[:, lane(N + 128 * j, 128)] = both_[:, 128:256]
+        both_ = nt(src[pl.ds(off, n * L), :], jnp.concatenate([wv[0, rows, :], wv[1, rows, :]], 0))
+        dst[pl.ds(0, n * L), lane(128 * j, 128)] = both_[:, 0:128]
+        dst[pl.ds(0, n * L), lane(N + 128 * j, 128)] = both_[:, 128:256]
 
     def scan(src, dst, groups, base, coef, reverse):
         e = 0 if reverse else 7
@@ -563,20 +565,20 @@
         z = jnp.zeros((8, 128), f32)
         return lax.fori_loop(0, L // 32, tile, (z,) * (2 * len(groups)))
 
-    def begin(src, off, dst, out, slot, j):
-        drive(src, off, dst, j)
-        fin = scan(dst, out, [(s * L, 128 * j) for s in range(S)], 0, True, False)
-        for s in range(S):
+    def begin(src, off, dst, out, slot, n, j):
+        drive(src, off, dst, n, j)
+        fin = scan(dst, out, [(s * L, 128 * j) for s in range(n)], 0, True, False)
+        for s in range(n):
             ce[slot, pl.ds(s, 1), lane(128 * j, 128)] = fin[2 * s][0:1, :]
-            ce[slot, pl.ds(S + s, 1), lane(128 * j, 128)] = fin[2 * s + 1][0:1, :]
-
-    def rest(*what):
+            ce[slot, pl.ds(n + s, 1), lane(128 * j, 128)] = fin[2 * s + 1][0:1, :]
+
+    def rest(what, tiles_=2):
         def step(k, _):
-            begin(*what, 1 + k * (1 - 2 * half))
+            begin(*what, 1 + k * (1 - 2 * half) if tiles_ == 2 else k)
             return 0
 
-        lax.fori_loop(0, 2, step, 0)
-        slot = what[4 - 0]
+        lax.fori_loop(0, tiles_, step, 0)
+        slot = what[4]
         return [remote(ce.at[slot], cer.at[slot, k], p) for k, p in enumerate(cpeer)]
 
     def incoming(slot, cps, n, forward):
@@ -600,16 +602,16 @@
     def entering(slot, k, lanes):
         return jnp.broadcast_to(cin[slot, pl.ds(k, 1), lanes], (8, 128))
 
-    def fix_batch(ref, dst, slot, keep):
+    def fix_batch(ref, dst, slot, keep, n):
         def fix_lanes(j, _):
             lr_, li_ = lane(128 * j, 128), lane(N + 128 * j, 128)
             p0, p1 = cst[6, :, lr_], cst[7, :, lr_]
             e0, e1 = cst[16, :, lr_], cst[17, :, lr_]
-            q0 = tuple(entering(slot, k * S + s, lr_) for s in range(S) for k in range(2))
+            q0 = tuple(entering(slot, k * n + s, lr_) for s in range(n) for k in range(2))
 
             def tile(i, q):
                 q = list(q)
-                for s in range(S):
+                for s in range(n):
                     rr, ri = [], []
                     for h in range(2):
                         rows = rows_at(s * L + i * 16 + 8 * h, 8)
@@ -631,8 +633,8 @@
 
         lax.fori_loop(0, N // 128, fix_lanes, 0)
 
-    def each_seq(f):
-        f(pl.ds(0, R))
+    def each_seq(f, n=S):
+        f(pl.ds(0, n * L))
 
     def tiles(f, lo=0, hi=R // 32):
         def step(i, _):
@@ -649,7 +651,8 @@
     def logistic(v):
         return 0.5 + 0.5 * jnp.tanh(0.5 * v)
 
-    batches = [(nrm, 0, raw, st, 0)] + [(nrme, R * k, rawe.at[k], rawe.at[k], 1 + k) for k in range(len(erank))]
+    batches = [(nrm, 0, raw, st, 0, S)] + [
+        (nrme, eoff[k], rawe.at[k], rawe.at[k], 1 + k, extra[k]) for k in range(len(extra))]
     arrived(*w3b)
     begin(*batches[0], 2 * half)
     w2c = spread(w4.at[qc, pair, :, wl], *far_c)
@@ -657,13 +660,13 @@
     og.append(cot_send(1))
     for cp in cxe:
         cp.wait()
-    lax.fori_loop(0, R // 128, lne_tile, 0)
+    lax.fori_loop(0, extra[0] * L // 128, lne_tile, 0)
     arrived(*w2b)
     w3b2 = remote(w4.at[0:2, pair, :, dl], w4.at[0:2, pair, :, dl], sib)
     og.append(cot_send(2))
     begin(*batches[1], 2 * half)
     arrived(w3b2)
-    fce = [rest(*batches[0])]
+    fce = [rest(batches[0])]
     arrived(near_c)
     w3c.append(remote(w4.at[2:4, t1, :, dl], w4.at[2:4, t1, :, dl], sib))
     arrived(near_g)
@@ -674,12 +677,11 @@
     arrived(*w2g)
     blk = gt.at[dr_, pairl]
     w3g.append(remote(blk, blk, sib))
-    fce.append(rest(*batches[1]))
-    if len(erank) > 1:
-        lax.fori_loop(R // 128, 2 * R // 128, lne_tile, 0)
-        begin(*batches[2], 2 * half)
+    fce.append(rest(batches[1]))
+    if len(extra) > 1:
+        lax.fori_loop(eoff[1] // 128, (eoff[1] + extra[1] * L) // 128, lne_tile, 0)
     incoming(0, fce[0], S, True)
-    fix_batch(st, sb, 0, True)
+    fix_batch(st, sb, 0, True, S)
     arrived(*w3c)
 
     def ssm_own(rows):
@@ -710,7 +712,12 @@
         ob[rows, :] = o.astype(bf16)
 
     tiles(out_tile)
-    outc = [remote(ob.at[:, lane(U * q, U)], out_hbm.at[mine, :], p) for q, p in ((t1, z1), (t3, z3))]
+    outc = [remote(ob.at[:, lane(U * t1, U)], out_hbm.at[mine, :], z1)]
+    done3 = extra[1] if len(extra) > 1 else 0
+    if done3 < S:
+        part = pl.ds(done3 * L, (S - done3) * L)
+        there3 = pl.ds(pl.multiple_of(R * t + done3 * L, L), (S - done3) * L)
+        outc.append(remote(ob.at[part, lane(U * t3, U)], out_hbm.at[there3, :], z3))
     locals_ = [local(ob.at[:, tl], out_hbm.at[mine, :])]
 
     def fold(v):
@@ -812,9 +819,10 @@
         accv[2] += lax.fori_loop(0, L // 128, tok_tile, jnp.zeros((8, H), f32))
         there = rows_at(R * t + L * s, L)
         locals_.append(local(tgb.at[rows, tl], tg_hbm.at[there, :]))
-        return [remote(tgb.at[rows, lane(U * p[2], U)], tg_hbm.at[there, :], p) for p in zpeer]
-
-    bs = [back_one(s) for s in range(S)]
+
+    def tok_send(s):
+        there = rows_at(R * t + L * s, L)
+        return [remote(tgb.at[pl.ds(s * L, L), lane(U * p[2], U)], tg_hbm.at[there, :], p) for p in (z3, z2, z1)]
 
     gcf, gbf = gc.reshape(2 * N, H), gb.reshape(2 * N, H)
     ol = lane(HD * (1 - d), HD)
@@ -823,15 +831,9 @@
         gcf[rows_at(j * 256, 256), :] = tn(sb[:, lane(j * 256, 256)], plb[...]).astype(bf16)
         return 0
 
-    lax.fori_loop(0, 2 * N // 256, gc_step, 0)
-    d1c = remote(gc.at[:, :, :, ol], r1c, sib)
-
     def gg_step(j, _):
         gg[rows_at(j * 256, 256), :] = tn(act[:, lane(j * 256, 256)], gl[...]).astype(bf16)
         return 0
-
-    lax.fori_loop(0, H // 256, gg_step, 0)
-    d1g = remote(gg.at[rows_at(HD * (1 - d), HD), :], r1g, sib)
 
     def gb_step(j, _):
         gbf[rows_at(j * 256, 256), :] = tn(nb[:, lane(j * 256, 256)], nrm[...]).astype(bf16)
@@ -869,26 +871,30 @@
         s3[1] = add2(s2[t2], r3[1])
         return remote(s3.at[1], r4, z2)
 
-    def five(d4, s3, r4, out):
+    def spread_out(stage, out):
+        locals_.append(local(stage, out.at[c]))
+        return [remote(stage, out.at[c], p) for p in cpeer]
+
+    def five(d4, s3, r4, stage, out):
         arrived(d4)
-        out[c] = add2(s3[0], r4[...])
-        return [remote(out.at[c], out.at[c], p) for p in cpeer]
+        stage[...] = add2(s3[0], r4[...])
+        return spread_out(stage, out)
 
     def extra_fix(k):
-        incoming(1 + k, fce[1 + k], S, True)
-        fix_batch(rawe.at[k], sbe, 1 + k, False)
+        incoming(1 + k, fce[1 + k], extra[k], True)
+        fix_batch(rawe.at[k], sbe, 1 + k, False, extra[k])
 
     def extra_act(k):
         def ssm(rows):
             tmpe[rows, :] = nn(sbe[rows, :], w4[2:4].reshape(2 * N, H))
 
-        each_seq(ssm)
+        each_seq(ssm, extra[k])
 
         def gelu(i, rows):
-            pre = tmpe[rows, :] + skip_r * nrme[rows_at(R * k + i * 32, 32), :].astype(f32)
+            pre = tmpe[rows, :] + skip_r * nrme[rows_at(eoff[k] + i * 32, 32), :].astype(f32)
             acte[rows, :] = (pre * (0.5 + 0.5 * jnp.tanh(pre * (SQ2PI + (SQ2PI * 0.044715) * (pre * pre))))).astype(bf16)
 
-        tiles(gelu)
+        tiles(gelu, 0, extra[k] * L // 32)
 
     def extra_out(k):
         rank = erank[k]
@@ -896,92 +902,72 @@
         def gate(rows):
             tmpe[rows, 0:U] = nn(acte[rows, :], gt[:, tl])
 
-        each_seq(gate)
+        each_seq(gate, extra[k])
         bias_u = jnp.sum(jnp.where(lax.broadcasted_iota(jnp.int32, (T, U), 0) == t, bias_t, 0.0), 0, keepdims=True)
 
         def fin(i, rows):
-            here = rows_at(R * k + i * 32, 32)
+            here = rows_at(eoff[k] + i * 32, 32)
             sg = logistic(tmpe[rows, 0:U] + bias_u)
             o = valid_of(i, rank) * (xe[here, tl].astype(f32) + acte[rows, tl].astype(f32) * sg)
             obe[here, :] = o.astype(bf16)
 
-        tiles(fin)
-        locals_.append(local(obe.at[pl.ds(R * k, R)], out_hbm.at[rows_at(R * rank, R), :]))
+        tiles(fin, 0, extra[k] * L // 32)
+        locals_.append(local(
+            obe.at[pl.ds(eoff[k], extra[k] * L)], out_hbm.at[pl.ds(pl.multiple_of(R * rank, R), extra[k] * L), :]))
 
     bias_t = jnp.concatenate([bias_r[:, U * k:U * k + U] for k in range(T)], 0)
-    tgc = back_two(0, bs[0])
+    bs, tgc = [], []
+    bs.append(back_one(0))
+    bs.append(back_one(1))
+    bs.append(back_one(2))
+    lax.fori_loop(0, 2 * N // 256, gc_step, 0)
+    d1c = remote(gc.at[:, :, :, ol], r1c, sib)
+    lax.fori_loop(0, H // 256, gg_step, 0)
+    d1g = remote(gg.at[rows_at(HD * (1 - d), HD), :], r1g, sib)
+    back_two(0, bs[0])
+    tgc += tok_send(0)
     d2c = two_states(gc, d1c, r1c, s1c, r2c)
     arrived(d1g)
     s1g[...] = add2(gg[dr_, :], r1g[...])
     d2g = [remote(s1g.at[gr(p[1]), :], r2g.at[k], p) for k, p in enumerate(cpeer)]
-    for k in range(1, S):
-        tgc += back_two(k, bs[k])
+    back_two(1, bs[1])
+    tgc += tok_send(1)
+    back_two(2, bs[2])
+    tgc += tok_send(2)
     lax.fori_loop(0, 2 * N // 256, gb_step, 0)
     d1b = remote(gb.at[:, :, :, ol], r1b, sib)
     for k, row in ((2, 0), (1, 1), (0, 2)):
         vv[row:row + 1, :] = jnp.sum(accv[k], 0, keepdims=True)
     d1v = remote(vv, vr1, sib)
-    if erank:
-        extra_fix(0)
+    extra_fix(0)
     d2b = two_states(gb, d1b, r1b, s1b, r2b)
     arrived(d1v)
     vr2[0] = vv[...] + vr1[...]
     d2v = [remote(vr2.at[0], vr2.at[k + 1], p) for k, p in enumerate(cpeer)]
-    if len(erank) > 1:
-        fce.append(rest(*batches[2]))
     d3c = three_states(d2c, s1c, r2c, s2c, r3c)
     arrived(*d2g)
     s2g[...] = total(s1g[gr(c), :], r2g, C - 1).astype(bf16)
     d3g = [remote(s2g.at[:, gl1], r3g.at[0], z1), remote(s2g.at[:, lane(U * t3, U)], r3g.at[1], z1)]
-    if erank:
-        extra_act(0)
+    extra_act(0)
     d4c = four_states(d3c, s2c, r3c, s3c, r4c)
     arrived(*d3g)
     s3g[0] = add2(s2g[:, tl], r3g[0])
     s3g[1] = add2(s2g[:, gl2], r3g[1])
     d4g = remote(s3g.at[1], r4g, z2)
-    if erank:
-        extra_out(0)
+    extra_out(0)
     arrived(*d2b)
     s2b[...] = total(s1b[rs_ctx(c)[0], :, rs_ctx(c)[1], :], r2b, C - 1).astype(bf16)
     d3b = [remote(s2b.at[p[2]], r3b.at[k], p) for k, p in enumerate(zpeer)]
     arrived(*d2v)
-    vr3[0] = vr2[0] + vr2[1] + vr2[2] + vr2[3]
-    d3v = [remote(vr3.at[0], vr3.at[k + 1], p) for k, p in enumerate(zpeer)]
-    if len(erank) > 1:
-        extra_fix(1)
-    d5 = five(d4c, s3c, r4c, fc_ref) + five(d4g, s3g, r4g, fg_ref)
-    if len(erank) > 1:
-        extra_act(1)
+    vr3[...] = vr2[0] + vr2[1] + vr2[2] + vr2[3]
+    locals_.append(local(vr3, fv_hbm.at[0]))
+    d3v = [remote(vr3, fv_hbm.at[k + 1], p) for k, p in enumerate(zpeer)]
+    d5 = five(d4c, s3c, r4c, q5c, fc_hbm) + five(d4g, s3g, r4g, q5g, fg_hbm)
     arrived(*d3b)
-    fb_ref[c] = total(s2b[t], r3b, T - 1).astype(bf16)
-    d5 += [remote(fb_ref.at[c], fb_ref.at[c], p) for p in cpeer]
-    if len(erank) > 1:
-        extra_out(1)
-
-    arrived(*d3v)
-    vf[...] = vr3[0] + vr3[1] + vr3[2] + vr3[3]
-    place = t * D + d
-    back = lambda n: lax.rem(H - n * place, H)
-    st8 = pltpu.roll(vf[...], back(NS // D), 1)[:, 0:NS // D]
-    ub8 = pltpu.roll(vf[...], back(U // D), 1)[:, 0:U // D]
-    lr1, li1, step1 = lre_in[...], lim_in[...], jnp.exp(stp_in[...])
-    dr1, di1, cr1, ci1 = (sm_ref[k:k + 1, 0:NS // D] for k in range(4))
-    gdr, gdi, gcr, gci = (st8[k:k + 1] for k in range(3, 7))
-    inv = 1.0 / (lr1 * lr1 + li1 * li1)
-    hdr = gdr + (gcr * lr1 - gci * li1) * inv
-    hdi = gdi + (gcr * li1 + gci * lr1) * inv
-    pull = 2.0 * (gcr * cr1 + gci * ci1)
-    e1, e2 = dr1 - 1.0, hdr * dr1 + hdi * di1
-    e3 = hdi * dr1 - hdr * di1
-    fv_ref[...] = jnp.zeros_like(fv_ref)
-    fv_ref[0:1, :] = vf[0:1, dl]
-    fv_ref[1:2, :] = vf[1:2, dl]
-    fv_ref[2:3, 0:U // D] = ub8[2:3]
-    fv_ref[3:4, 0:NS // D] = (gcr * e1 + gci * di1 - pull * lr1) * inv + step1 * e2
-    fv_ref[4:5, 0:NS // D] = (gcr * di1 - gci * e1 - pull * li1) * inv + step1 * e3
-    fv_ref[5:6, 0:NS // D] = step1 * (lr1 * e2 + li1 * e3)
-    arrived(*d5, *tgc, *outc)
+    q5b[...] = total(s2b[t], r3b, T - 1).astype(bf16)
+    d5 += spread_out(q5b, fb_hbm)
+
+    arrived(*d5, *d3v, *tgc, *outc)
     for cp in locals_:
         cp.wait()
     for cp in started:
@@ -989,7 +975,8 @@
     assert count[0] == NSEM and nlocal[0] == NLOCAL, (count[0], nlocal[0])
 
 
-NSEM, NLOCAL = 106, 19
+EXTRA = (3,)
+NSEM, NLOCAL = 106, 23
 
 
 def fused_call(geo, lens, x2, og2, *params):
@@ -998,7 +985,7 @@
     f32, bf16 = jnp.float32, jnp.bfloat16
     uq, hs = HD // C, NS // 2
     V = pltpu.VMEM
-    any_, vm = pl.BlockSpec(memory_space=pl.ANY), pl.BlockSpec(memory_space=pltpu.VMEM)
+    any_ = pl.BlockSpec(memory_space=pl.ANY)
     scratch = [
         V((R, H), bf16), V((R, H), bf16), V((R, H), f32), V((R, 128), f32),
         V((R, 2 * N), f32), V((R, 2 * N), f32), V((R, 2 * N), bf16),
@@ -1016,20 +1003,21 @@
         V((T, hs, HD), bf16), V((uq, H), bf16), V((T, hs, HD), bf16),
         V((2, hs, HD), bf16), V((2, uq, U), bf16), V((T - 1, hs, HD), bf16),
         V((2, hs, HD), bf16), V((2, uq, U), bf16), V((hs, HD), bf16), V((uq, U), bf16),
-        V((8, H), f32), V((8, H), f32), V((C, 8, H), f32), V((T, 8, H), f32), V((8, H), f32), V((3, 8, H), f32),
+        V((hs, HD), bf16), V((uq, U), bf16), V((hs, HD), bf16),
+        V((8, H), f32), V((8, H), f32), V((C, 8, H), f32), V((8, H), f32), V((3, 8, H), f32),
         V((4, NS, HD), bf16), V((8, HD), f32), V((HD, U), bf16), V((1, HD), f32), V((1, HD), f32),
         V((1, NS // D), f32), V((1, NS // D), f32), V((1, NS // D), f32), V((1, U // D), f32),
         pltpu.SemaphoreType.DMA((NLOCAL,)), pltpu.SemaphoreType.DMA((NSEM,)), pltpu.SemaphoreType.DMA((NSEM,)),
     ]
     rows = x2.shape[0]
     return pl.pallas_call(
-        functools.partial(fused_body, geo),
+        functools.partial(fused_body, geo, EXTRA),
         out_shape=(
             jax.ShapeDtypeStruct((rows, U), bf16), jax.ShapeDtypeStruct((rows, U), bf16),
             jax.ShapeDtypeStruct((C, hs, HD), bf16), jax.ShapeDtypeStruct((C, uq, U), bf16),
-            jax.ShapeDtypeStruct((C, hs, HD), bf16), jax.ShapeDtypeStruct((8, HD), f32)),
+            jax.ShapeDtypeStruct((C, hs, HD), bf16), jax.ShapeDtypeStruct((T, 8, H), f32)),
         in_specs=[pl.BlockSpec(memory_space=pltpu.SMEM), any_, any_] + [any_] * 11,
-        out_specs=(any_, any_, vm, vm, vm, vm),
+        out_specs=(any_,) * 6,
         scratch_shapes=scratch,
         compiler_params=pltpu.CompilerParams(
             collective_id=0, has_side_effects=True, vmem_limit_bytes=60 * 1024 * 1024),
@@ -1037,12 +1025,16 @@
     )(lens, x2, og2, *params)
 
 
-def finish_body(geo, len_ref, out_in, tok_in, og_in, fc_in, fg_in, fb_in, fv, out, ingrad, gain_g, skip_g,
-                lre_g, lim_g, step_g, bre_g, bim_g, cre_g, cim_g, glu_g, bias_g,
-                tokv, ogv, outv, fc, fg, fb, bre, bim, cre, cim, glu, res, sem, gsem, osem):
+def finish_body(geo, len_ref, out_in, tok_in, og_in, fc_in, fg_in, fb_in, fv_in, lre_in, lim_in, stp_in, *refs):
     D, C, T, S, L, H, N, U = geo
     NS = N // T
     f32 = jnp.float32
+    out, ingrad = refs[:2]
+    small_out, big_out = refs[2:8], refs[8:13]
+    tokv, ogv, outv, fc, fg, fb, fv, lre, lim, stp = refs[13:23]
+    small, big = refs[23:29], refs[29:34]
+    res, vf, sem, gsem, osem = refs[34:]
+    d, c, t = lax.axis_index("dp"), lax.axis_index("ctx"), lax.axis_index("tp")
 
     def move(src, dst, s):
         cp = pltpu.make_async_copy(src, dst, s)
@@ -1052,68 +1044,80 @@
     part = [pl.ds(S * k, S) for k in range(T)]
     loads = [(move(tok_in.at[part[k]], tokv.at[part[k]], sem.at[0, k]),
               move(og_in.at[part[k]], ogv.at[part[k]], sem.at[1, k])) for k in range(T)]
-    params = [move(a, b, gsem.at[k]) for k, (a, b) in enumerate(((fc_in, fc), (fg_in, fg), (fb_in, fb)))]
+    params = [move(a, b, gsem.at[k]) for k, (a, b) in enumerate((
+        (fv_in, fv), (lre_in, lre), (lim_in, lim), (stp_in, stp), (fc_in, fc), (fg_in, fg), (fb_in, fb)))]
     passes = [move(out_in.at[part[k]], outv.at[part[k]], sem.at[2, k]) for k in range(T)]
-    base = lax.axis_index("ctx") * L
+    pos = c * L + lax.broadcasted_iota(jnp.int32, (L, 1), 0)
     stores = []
     for k in range(T):
         for cp in loads[k]:
             cp.wait()
-
-        def tile(i, _):
-            s = S * k + i // (L // 32)
-            r0 = lax.rem(i, L // 32) * 32
-            rows = pl.ds(pl.multiple_of(r0, 32), 32)
-            pos = base + r0 + lax.broadcasted_iota(jnp.int32, (32, 1), 0)
+        for s in range(S * k, S * k + S):
             keep = jnp.where(pos < len_ref[s], 1.0, 0.0)
-            res[s, rows, :] = keep * ogv[s, rows, :].astype(f32) + tokv[s, rows, :].astype(f32)
-            return 0
-
-        lax.fori_loop(0, S * L // 32, tile, 0)
+            res[s] = keep * ogv[s].astype(f32) + tokv[s].astype(f32)
         stores.append(move(res.at[part[k]], ingrad.at[part[k]], osem.at[k]))
     for cp in params:
         cp.wait()
     h = C // 2
     for k in range(C):
         rows = pl.ds((k % h) * (NS // h), NS // h)
-        (bre if k < h else bim)[rows, :] = fb[k].astype(f32)
-        (cre if k < h else cim)[rows, :] = fc[k].astype(f32)
-    glu[...] = fg[...].reshape(glu.shape).astype(f32)
-    pairs = ((bre, bre_g), (bim, bim_g), (cre, cre_g), (cim, cim_g), (glu, glu_g))
-    stores += [move(a, b, osem.at[2 * T + k]) for k, (a, b) in enumerate(pairs)]
+        big[0 if k < h else 1][rows, :] = fb[k].astype(f32)
+        big[2 if k < h else 3][rows, :] = fc[k].astype(f32)
+    big[4][...] = fg[...].reshape(big[4].shape).astype(f32)
+    stores += [move(a, b, osem.at[2 * T + k]) for k, (a, b) in enumerate(zip(big, big_out))]
     for k in range(T):
         passes[k].wait()
         stores.append(move(outv.at[part[k]], out.at[part[k]], osem.at[T + k]))
-    gain_g[...] = fv[0:1, :]
-    skip_g[...] = fv[1:2, :]
-    bias_g[...] = fv[2:3, 0:U // D]
-    lre_g[...] = fv[3:4, 0:NS // D]
-    lim_g[...] = fv[4:5, 0:NS // D]
-    step_g[...] = fv[5:6, 0:NS // D]
+    acc = fv[0]
+    for k in range(1, T):
+        acc = acc + fv[k]
+    vf[...] = acc
+    place = t * D + d
+    back = lambda n: lax.rem(H - n * place, H)
+    st8 = pltpu.roll(acc, back(NS // D), 1)[:, 0:NS // D]
+    ub8 = pltpu.roll(acc, back(U // D), 1)[:, 0:U // D]
+    lr1, li1 = lre[...], lim[...]
+    dr1, di1, cr1, ci1 = coefficients(lr1, li1, stp[...])
+    step1 = jnp.exp(stp[...])
+    gdr, gdi, gcr, gci = (st8[k:k + 1] for k in range(3, 7))
+    inv = 1.0 / (lr1 * lr1 + li1 * li1)
+    hdr = gdr + (gcr * lr1 - gci * li1) * inv
+    hdi = gdi + (gcr * li1 + gci * lr1) * inv
+    pull = 2.0 * (gcr * cr1 + gci * ci1)
+    e1, e2 = dr1 - 1.0, hdr * dr1 + hdi * di1
+    e3 = hdi * dr1 - hdr * di1
+    dl = lane(H // D * d, H // D)
+    small[0][...] = vf[0:1, dl]
+    small[1][...] = vf[1:2, dl]
+    small[2][...] = (gcr * e1 + gci * di1 - pull * lr1) * inv + step1 * e2
+    small[3][...] = (gcr * di1 - gci * e1 - pull * li1) * inv + step1 * e3
+    small[4][...] = step1 * (lr1 * e2 + li1 * e3)
+    small[5][...] = ub8[2:3]
+    stores += [move(a, b, osem.at[2 * T + 5 + k]) for k, (a, b) in enumerate(zip(small, small_out))]
     for cp in stores:
         cp.wait()
 
 
-def finish_call(geo, lens, out, tok, og, fc, fg, fb, fv):
+def finish_call(geo, lens, out, tok, og, fc, fg, fb, fv, lre, lim, stp):
     D, C, T, S, L, H, N, U = geo
     NS, HD = N // T, H // D
     f32, bf16 = jnp.float32, jnp.bfloat16
     seqs = S * T
-    any_, vm = pl.BlockSpec(memory_space=pl.ANY), pl.BlockSpec(memory_space=pltpu.VMEM)
+    any_ = pl.BlockSpec(memory_space=pl.ANY)
     V = pltpu.VMEM
-    small = [(1, HD), (1, HD)] + [(1, NS // D)] * 3 + [(NS, HD)] * 4 + [(HD, U), (1, U // D)]
+    sizes = [(1, HD), (1, HD)] + [(1, NS // D)] * 3 + [(1, U // D)] + [(NS, HD)] * 4 + [(HD, U)]
     return pl.pallas_call(
         functools.partial(finish_body, geo),
         out_shape=[jax.ShapeDtypeStruct((seqs, L, U), bf16), jax.ShapeDtypeStruct((seqs, L, U), f32)]
-        + [jax.ShapeDtypeStruct(s, f32) for s in small],
-        in_specs=[pl.BlockSpec(memory_space=pltpu.SMEM)] + [any_] * 6 + [vm],
-        out_specs=[any_, any_] + [vm] * 5 + [any_] * 5 + [vm],
-        scratch_shapes=[V((seqs, L, U), bf16)] * 3 + [V(a.shape, a.dtype) for a in (fc, fg, fb)]
-        + [V((NS, HD), f32)] * 4 + [V((HD, U), f32), V((seqs, L, U), f32)]
-        + [pltpu.SemaphoreType.DMA((3, T)), pltpu.SemaphoreType.DMA((3,)), pltpu.SemaphoreType.DMA((2 * T + 5,))],
+        + [jax.ShapeDtypeStruct(s, f32) for s in sizes],
+        in_specs=[pl.BlockSpec(memory_space=pltpu.SMEM)] + [any_] * 10,
+        out_specs=[any_] * 13,
+        scratch_shapes=[V((seqs, L, U), bf16)] * 3 + [V(a.shape, a.dtype) for a in (fc, fg, fb, fv, lre, lim, stp)]
+        + [V(s, f32) for s in sizes] + [V((seqs, L, U), f32), V((8, H), f32)]
+        + [pltpu.SemaphoreType.DMA((3, T)), pltpu.SemaphoreType.DMA((7,)), pltpu.SemaphoreType.DMA((2 * T + 11,))],
         compiler_params=pltpu.CompilerParams(vmem_limit_bytes=60 * 1024 * 1024),
         name="finish",
-    )(lens, out.reshape(seqs, L, U), tok.reshape(seqs, L, U), og, fc, fg, fb, fv)
+    )(lens, out.reshape(seqs, L, U), tok.reshape(seqs, L, U), og, fc, fg, fb, fv, lre, lim, stp)
 
 
 def coefficients(lam_re, lam_im, step_log):
@@ -1134,13 +1138,12 @@
     NS, HD = b_re.shape
     U = glu_weight.shape[1]
     geo = (D, C, T, seqs // T, L, H, NS * T, U)
-    row = lambda v: v.reshape(1, -1)
+    rows = [v.reshape(1, -1) for v in (norm_gain, skip_weight, lambda_re, lambda_im, log_step, glu_bias)]
     out, tok, fc, fg, fb, fv = fused_call(
         geo, lengths, inputs.reshape(seqs * L, H), out_grad.reshape(seqs * L, U),
-        b_re, b_im, c_re.T, c_im.T, glu_weight,
-        *(row(v) for v in (norm_gain, skip_weight, lambda_re, lambda_im, log_step, glu_bias)))
-    res = finish_call(geo, lengths, out, tok, out_grad, fc, fg, fb, fv)
-    out, ingrad, gain_g, skip_g, lre_g, lim_g, step_g, bre_g, bim_g, cre_g, cim_g, glu_g, bias_g = res
+        b_re, b_im, c_re.T, c_im.T, glu_weight, *rows)
+    res = finish_call(geo, lengths, out, tok, out_grad, fc, fg, fb, fv, *rows[2:5])
+    out, ingrad, gain_g, skip_g, lre_g, lim_g, step_g, bias_g, bre_g, bim_g, cre_g, cim_g, glu_g = res
     flat = lambda v: v.reshape(-1)
     return (out, ingrad, flat(gain_g), flat(skip_g), flat(lre_g), flat(lim_g), flat(step_g),
             bre_g, bim_g, cre_g.T, cim_g.T, glu_g, flat(bias_g))

time: 75.6 us -> 73.7 us (0.975)
  Pallas kernels: 74.7 us -> 72.8 us
    pallas_call x1, Pallas kernels: 5.28 us -> 3.88 us  [finish_call(): pl.pallas_call(functools.partial(finish_body, geo), out_shape=[jax.ShapeD...]
where the time goes in v2:
time: 73.7 us; the launch traced here: 73.5 us
  Pallas kernels  72.8 us (99%)
    pallas_call x1, Pallas kernels, fused_call(): pl.pallas_call(functools.partial(fused_body, geo, EXTRA), out_shape=(jax....  68.9 us
    pallas_call x1, Pallas kernels, finish_call(): pl.pallas_call(functools.partial(finish_body, geo), out_shape=[jax.ShapeD...  3.88 us

profile of v2, /device:TPU:0, one launch (start us, length us, event | category | flops | bytes accessed | tf_op | source)
XLA Modules:
  0.0 73.5 jit_solution(16341966717532374256)
XLA Ops:
  0.6 68.9 %block.1 = (bf16[3072,128]{1,0:T(8,128)(2,1)}, bf16[3072,128]{1,0:T(8,128)(2,1)}, bf16[4,48,256]{2,1,0:T(8,128)(2,1)}, bf16[4,64,128]{2,1,0:T(8,128)(2,1)}, bf16...) custom-call(s32[12]{0:T(128)} %len_ref.1, bf16[3072,512]{1,0:T(8,128)(2,1)} %bitcast.20, bf16[3072,128]{1,0:T(8,128)(2,1)} %bitcast.21, ...), custom_call_target="tpu_custom_call" | custom-call | tf_op jit(solution)/shard_map/block/pallas_call | solution.py:1013
  69.6 3.9 %finish.1 = (bf16[12,256,128]{2,1,0:T(8,128)(2,1)}, f32[12,256,128]{2,1,0:T(8,128)}, f32[1,256]{1,0:T(1,128)}, f32[1,256]{1,0:T(1,128)}, f32[1,48]{1,0:T(1,128)}...) custom-call(s32[12]{0:T(128)} %len_ref.1, ...), custom_call_target="tpu_custom_call" | custom-call | tf_op jit(solution)/shard_map/finish/pallas_call | solution.py:1109

commit v3 on v2

--- a/solution.py
+++ b/solution.py
@@ -678,8 +678,6 @@
     blk = gt.at[dr_, pairl]
     w3g.append(remote(blk, blk, sib))
     fce.append(rest(batches[1]))
-    if len(extra) > 1:
-        lax.fori_loop(eoff[1] // 128, (eoff[1] + extra[1] * L) // 128, lne_tile, 0)
     incoming(0, fce[0], S, True)
     fix_batch(st, sb, 0, True, S)
     arrived(*w3c)
@@ -919,19 +917,19 @@
     bs, tgc = [], []
     bs.append(back_one(0))
     bs.append(back_one(1))
+    back_two(0, bs[0])
+    tgc += tok_send(0)
     bs.append(back_one(2))
     lax.fori_loop(0, 2 * N // 256, gc_step, 0)
     d1c = remote(gc.at[:, :, :, ol], r1c, sib)
     lax.fori_loop(0, H // 256, gg_step, 0)
     d1g = remote(gg.at[rows_at(HD * (1 - d), HD), :], r1g, sib)
-    back_two(0, bs[0])
-    tgc += tok_send(0)
     d2c = two_states(gc, d1c, r1c, s1c, r2c)
+    back_two(1, bs[1])
+    tgc += tok_send(1)
     arrived(d1g)
     s1g[...] = add2(gg[dr_, :], r1g[...])
     d2g = [remote(s1g.at[gr(p[1]), :], r2g.at[k], p) for k, p in enumerate(cpeer)]
-    back_two(1, bs[1])
-    tgc += tok_send(1)
     back_two(2, bs[2])
     tgc += tok_send(2)
     lax.fori_loop(0, 2 * N // 256, gb_step, 0)
@@ -939,22 +937,24 @@
     for k, row in ((2, 0), (1, 1), (0, 2)):
         vv[row:row + 1, :] = jnp.sum(accv[k], 0, keepdims=True)
     d1v = remote(vv, vr1, sib)
-    extra_fix(0)
     d2b = two_states(gb, d1b, r1b, s1b, r2b)
     arrived(d1v)
     vr2[0] = vv[...] + vr1[...]
     d2v = [remote(vr2.at[0], vr2.at[k + 1], p) for k, p in enumerate(cpeer)]
+    extra_fix(0)
+    extra_act(0)
     d3c = three_states(d2c, s1c, r2c, s2c, r3c)
     arrived(*d2g)
     s2g[...] = total(s1g[gr(c), :], r2g, C - 1).astype(bf16)
     d3g = [remote(s2g.at[:, gl1], r3g.at[0], z1), remote(s2g.at[:, lane(U * t3, U)], r3g.at[1], z1)]
-    extra_act(0)
+    extra_out(0)
+    lax.fori_loop(eoff[1] // 128, (eoff[1] + extra[1] * L) // 128, lne_tile, 0)
+    fce.append(rest(batches[2], N // 128))
     d4c = four_states(d3c, s2c, r3c, s3c, r4c)
     arrived(*d3g)
     s3g[0] = add2(s2g[:, tl], r3g[0])
     s3g[1] = add2(s2g[:, gl2], r3g[1])
     d4g = remote(s3g.at[1], r4g, z2)
-    extra_out(0)
     arrived(*d2b)
     s2b[...] = total(s1b[rs_ctx(c)[0], :, rs_ctx(c)[1], :], r2b, C - 1).astype(bf16)
     d3b = [remote(s2b.at[p[2]], r3b.at[k], p) for k, p in enumerate(zpeer)]
@@ -962,10 +962,13 @@
     vr3[...] = vr2[0] + vr2[1] + vr2[2] + vr2[3]
     locals_.append(local(vr3, fv_hbm.at[0]))
     d3v = [remote(vr3, fv_hbm.at[k + 1], p) for k, p in enumerate(zpeer)]
+    extra_fix(1)
     d5 = five(d4c, s3c, r4c, q5c, fc_hbm) + five(d4g, s3g, r4g, q5g, fg_hbm)
+    extra_act(1)
     arrived(*d3b)
     q5b[...] = total(s2b[t], r3b, T - 1).astype(bf16)
     d5 += spread_out(q5b, fb_hbm)
+    extra_out(1)
 
     arrived(*d5, *d3v, *tgc, *outc)
     for cp in locals_:
@@ -975,8 +978,8 @@
     assert count[0] == NSEM and nlocal[0] == NLOCAL, (count[0], nlocal[0])
 
 
-EXTRA = (3,)
-NSEM, NLOCAL = 106, 23
+EXTRA = (3, 1,)
+NSEM, NLOCAL = 109, 25
 
 
 def fused_call(geo, lens, x2, og2, *params):

time: 73.7 us -> 71.3 us (0.967)
  Pallas kernels: 72.8 us -> 70.4 us
    pallas_call x1, Pallas kernels: 68.9 us -> 66.6 us  [fused_call(): pl.pallas_call(functools.partial(fused_body, geo, EXTRA), out_shape=(jax....]
where the time goes in v3:
time: 71.3 us; the launch traced here: 71.1 us
  Pallas kernels  70.4 us (99%)
    pallas_call x1, Pallas kernels, fused_call(): pl.pallas_call(functools.partial(fused_body, geo, EXTRA), out_shape=(jax....  66.6 us
    pallas_call x1, Pallas kernels, finish_call(): pl.pallas_call(functools.partial(finish_body, geo), out_shape=[jax.ShapeD...  3.88 us

profile of v3, /device:TPU:0, one launch (start us, length us, event | category | flops | bytes accessed | tf_op | source)
XLA Modules:
  0.0 71.1 jit_solution(6809903273105158561)
XLA Ops:
  0.6 66.6 %block.1 = (bf16[3072,128]{1,0:T(8,128)(2,1)}, bf16[3072,128]{1,0:T(8,128)(2,1)}, bf16[4,48,256]{2,1,0:T(8,128)(2,1)}, bf16[4,64,128]{2,1,0:T(8,128)(2,1)}, bf16...) custom-call(s32[12]{0:T(128)} %len_ref.1, bf16[3072,512]{1,0:T(8,128)(2,1)} %bitcast.20, bf16[3072,128]{1,0:T(8,128)(2,1)} %bitcast.21, ...), custom_call_target="tpu_custom_call" | custom-call | tf_op jit(solution)/shard_map/block/pallas_call | solution.py:1016
  67.2 3.9 %finish.1 = (bf16[12,256,128]{2,1,0:T(8,128)(2,1)}, f32[12,256,128]{2,1,0:T(8,128)}, f32[1,256]{1,0:T(1,128)}, f32[1,256]{1,0:T(1,128)}, f32[1,48]{1,0:T(1,128)}...) custom-call(s32[12]{0:T(128)} %len_ref.1, ...), custom_call_target="tpu_custom_call" | custom-call | tf_op jit(solution)/shard_map/finish/pallas_call | solution.py:1112

commit v4 on v3

--- a/solution.py
+++ b/solution.py
@@ -917,6 +917,7 @@
     bs, tgc = [], []
     bs.append(back_one(0))
     bs.append(back_one(1))
+    extra_fix(0)
     back_two(0, bs[0])
     tgc += tok_send(0)
     bs.append(back_one(2))
@@ -941,13 +942,12 @@
     arrived(d1v)
     vr2[0] = vv[...] + vr1[...]
     d2v = [remote(vr2.at[0], vr2.at[k + 1], p) for k, p in enumerate(cpeer)]
-    extra_fix(0)
     extra_act(0)
+    extra_out(0)
     d3c = three_states(d2c, s1c, r2c, s2c, r3c)
     arrived(*d2g)
     s2g[...] = total(s1g[gr(c), :], r2g, C - 1).astype(bf16)
     d3g = [remote(s2g.at[:, gl1], r3g.at[0], z1), remote(s2g.at[:, lane(U * t3, U)], r3g.at[1], z1)]
-    extra_out(0)
     lax.fori_loop(eoff[1] // 128, (eoff[1] + extra[1] * L) // 128, lne_tile, 0)
     fce.append(rest(batches[2], N // 128))
     d4c = four_states(d3c, s2c, r3c, s3c, r4c)

time: 71.3 us -> 71.3 us (level)
  no operation moved by 1% of the time
where the time goes in v4:
time: 71.3 us; the launch traced here: 71.1 us
  Pallas kernels  70.4 us (99%)
    pallas_call x1, Pallas kernels, fused_call(): pl.pallas_call(functools.partial(fused_body, geo, EXTRA), out_shape=(jax....  66.6 us
    pallas_call x1, Pallas kernels, finish_call(): pl.pallas_call(functools.partial(finish_body, geo), out_shape=[jax.ShapeD...  3.88 us

profile of v4, /device:TPU:0, one launch (start us, length us, event | category | flops | bytes accessed | tf_op | source)
XLA Modules:
  0.0 71.1 jit_solution(16976023108417914752)
XLA Ops:
  0.6 66.6 %block.1 = (bf16[3072,128]{1,0:T(8,128)(2,1)}, bf16[3072,128]{1,0:T(8,128)(2,1)}, bf16[4,48,256]{2,1,0:T(8,128)(2,1)}, bf16[4,64,128]{2,1,0:T(8,128)(2,1)}, bf16...) custom-call(s32[12]{0:T(128)} %len_ref.1, bf16[3072,512]{1,0:T(8,128)(2,1)} %bitcast.20, bf16[3072,128]{1,0:T(8,128)(2,1)} %bitcast.21, ...), custom_call_target="tpu_custom_call" | custom-call | tf_op jit(solution)/shard_map/block/pallas_call | solution.py:1016
  67.2 3.9 %finish.1 = (bf16[12,256,128]{2,1,0:T(8,128)(2,1)}, f32[12,256,128]{2,1,0:T(8,128)}, f32[1,256]{1,0:T(1,128)}, f32[1,256]{1,0:T(1,128)}, f32[1,48]{1,0:T(1,128)}...) custom-call(s32[12]{0:T(128)} %len_ref.1, ...), custom_call_target="tpu_custom_call" | custom-call | tf_op jit(solution)/shard_map/finish/pallas_call | solution.py:1112
